TPU v7x, 32 devices: a whole 2x2x4 slice. The times are simulated.
32 devices in a mesh: dp: 4 (over y, x), seq: 8 (over z, core).
Axes of the slice: x: 2, y: 2, z: 4, core: 2. Of those that a mesh axis runs over, the one named last changes fastest.
Arguments:
- inputs: bfloat16 [4, 1024, 1600], P('dp', 'seq'), may hold values from -6 to 6
- segment_ids: int32 [4, 1024], P('dp', 'seq'), may hold values from 0 to 3, never falling along the last dimension, each value on 1 to 512 neighbouring positions
- cotangent: bfloat16 [4, 1024, 1600], P('dp', 'seq'), may hold values from -6 to 6
- attn_gain: bfloat16 [1600], P('seq'), may hold values from 0.5 to 1.5
- attn_shift: bfloat16 [1600], P('seq'), may hold values from -2 to 2
- qkv_weight: bfloat16 [1600, 4800], P('dp', 'seq'), may hold values from -0.15625 to 0.15625
- query_bias: bfloat16 [1600], P('seq'), may hold values from -2 to 2
- value_bias: bfloat16 [1600], P('seq'), may hold values from -2 to 2
- out_weight: bfloat16 [1600, 1600], P('dp', 'seq'), may hold values from -0.625 to 0.625
- out_bias: bfloat16 [1600], P('seq'), may hold values from -2 to 2
- mlp_gain: bfloat16 [1600], P('seq'), may hold values from 0.5 to 1.5
- mlp_shift: bfloat16 [1600], P('seq'), may hold values from -2 to 2
- up_weight: bfloat16 [1600, 6400], P('dp', 'seq'), may hold values from -0.15625 to 0.15625
- up_bias: bfloat16 [6400], P('seq'), may hold values from -2 to 2
- down_weight: bfloat16 [6400, 1600], P('dp', 'seq'), may hold values from -0.078125 to 0.078125
- down_bias: bfloat16 [1600], P('seq'), may hold values from -2 to 2
Outputs:
- output: bfloat16 [4, 1024, 1600], P('dp', 'seq')
- grad_inputs: float32 [4, 1024, 1600], P('dp', 'seq')
- grad_attn_gain: float32 [1600], P('seq')
- grad_attn_shift: float32 [1600], P('seq')
- grad_qkv_weight: float32 [1600, 4800], P('dp', 'seq')
- grad_query_bias: float32 [1600], P('seq')
- grad_value_bias: float32 [1600], P('seq')
- grad_out_weight: float32 [1600, 1600], P('dp', 'seq')
- grad_out_bias: float32 [1600], P('seq')
- grad_mlp_gain: float32 [1600], P('seq')
- grad_mlp_shift: float32 [1600], P('seq')
- grad_up_weight: float32 [1600, 6400], P('dp', 'seq')
- grad_up_bias: float32 [6400], P('seq')
- grad_down_weight: float32 [6400, 1600], P('dp', 'seq')
- grad_down_bias: float32 [1600], P('seq')
Inputs may be any that keep to these rules, and one draw needn't show every extreme that they name: `segment_ids`: along each sequence the ids never fall; each document holds 1 to 512 tokens, and some document holds exactly that many.
All inputs are finite; a program needn't handle non-finite values.
Results may differ from a plain program's by a relative error of at most 0.011.
Values may be sent and summed in bfloat16 or wider, within the bound.
A program may use at most 320 MiB of HBM per device.

v0:
```python
import jax
import jax.numpy as jnp
from jax import lax
from jax.sharding import PartitionSpec as P

HEADS = 25
HEAD_DIM = 64


def layer_norm(values, gain, shift):
    center = values - jnp.mean(values, axis=-1, keepdims=True)
    spread = jnp.mean(center * center, axis=-1, keepdims=True)
    return center * lax.rsqrt(spread + 1e-05) * gain + shift


def gelu_tanh(values):
    return jax.nn.gelu(values, approximate=True)


def contract_rows(left, right):
    return lax.dot_general(
        left, right, (((0,), (0,)), ((), ())), preferred_element_type=jnp.float32
    )


def contract_cols(left, right):
    return lax.dot_general(
        left, right, (((1,), (1,)), ((), ())), preferred_element_type=jnp.float32
    )


def masked_scores(query_heads, key_part, seg_query, pos_query, seg_key, pos_key, scaling):
    scores = (
        jnp.einsum("qhd,khd->hqk", query_heads, key_part, preferred_element_type=jnp.float32)
        * scaling
    )
    visible = (seg_query[:, None] == seg_key[None, :]) & (pos_key[None, :] <= pos_query[:, None])
    return jnp.where(visible[None], scores, -1e30)


def shards(
    inputs,
    segment_ids,
    cotangent,
    attn_gain,
    attn_shift,
    qkv_weight,
    query_bias,
    value_bias,
    out_weight,
    out_bias,
    mlp_gain,
    mlp_shift,
    up_weight,
    up_bias,
    down_weight,
    down_bias,
):
    rows = (
        lax.all_gather(qkv_weight, "dp", axis=0, tiled=True),
        lax.all_gather(out_weight, "dp", axis=0, tiled=True),
        lax.all_gather(up_weight, "dp", axis=0, tiled=True),
        lax.all_gather(down_weight, "dp", axis=0, tiled=True),
    )
    full = (
        lax.all_gather(rows[0], "seq", axis=1, tiled=True),
        lax.all_gather(rows[1], "seq", axis=1, tiled=True),
        lax.all_gather(rows[2], "seq", axis=1, tiled=True),
        lax.all_gather(rows[3], "seq", axis=1, tiled=True),
        lax.all_gather(attn_gain, "seq", axis=0, tiled=True),
        lax.all_gather(attn_shift, "seq", axis=0, tiled=True),
        lax.all_gather(query_bias, "seq", axis=0, tiled=True),
        lax.all_gather(value_bias, "seq", axis=0, tiled=True),
        lax.all_gather(out_bias, "seq", axis=0, tiled=True),
        lax.all_gather(mlp_gain, "seq", axis=0, tiled=True),
        lax.all_gather(mlp_shift, "seq", axis=0, tiled=True),
        lax.all_gather(up_bias, "seq", axis=0, tiled=True),
        lax.all_gather(down_bias, "seq", axis=0, tiled=True),
    )
    qkv_full, out_full, up_full, down_full = (full[0], full[1], full[2], full[3])
    vectors = [item.astype(jnp.float32) for item in full[4:]]
    (
        gain_one,
        shift_one,
        bias_query,
        bias_value,
        bias_out,
        gain_two,
        shift_two,
        bias_up,
        bias_down,
    ) = vectors
    width = inputs.shape[2]
    tok_count = inputs.shape[1]
    scaling = HEAD_DIM ** (-0.5)
    stream = inputs[0].astype(jnp.float32)
    normed_low = layer_norm(stream, gain_one, shift_one).astype(jnp.bfloat16)
    biases = jnp.concatenate([bias_query, jnp.zeros_like(bias_query), bias_value])
    mixed = (jnp.dot(normed_low, qkv_full, preferred_element_type=jnp.float32) + biases).astype(
        jnp.bfloat16
    )
    queries = mixed[:, :width]
    own_keys = mixed[:, width : 2 * width]
    own_values = mixed[:, 2 * width :]
    seg_query = segment_ids[0]
    gathered = (
        lax.all_gather(own_keys, "seq", axis=0, tiled=True),
        lax.all_gather(own_values, "seq", axis=0, tiled=True),
        lax.all_gather(seg_query.astype(jnp.bfloat16), "seq", axis=0, tiled=True),
    )
    seq_length = gathered[0].shape[0]
    span = min(512, seq_length)
    blocks_total = seq_length // span
    key_rows = gathered[0].reshape(blocks_total, span, HEADS, HEAD_DIM)
    value_rows = gathered[1].reshape(blocks_total, span, HEADS, HEAD_DIM)
    seg_keys = gathered[2].astype(jnp.int32).reshape(blocks_total, span)
    pos_keys = jnp.arange(seq_length, dtype=jnp.int32).reshape(blocks_total, span)
    pos_query = lax.axis_index("seq") * tok_count + jnp.arange(tok_count, dtype=jnp.int32)
    query_heads = queries.reshape(tok_count, HEADS, HEAD_DIM)
    key_blocks = (key_rows, value_rows, seg_keys, pos_keys)

    def max_step(state_pair, portion):
        row_top, row_total = state_pair
        scores = masked_scores(
            query_heads, portion[0], seg_query, pos_query, portion[2], portion[3], scaling
        )
        new_top = jnp.maximum(row_top, jnp.max(scores, axis=-1))
        row_total = row_total * jnp.exp(row_top - new_top) + jnp.sum(
            jnp.exp(scores - new_top[..., None]), axis=-1
        )
        return ((new_top, row_total), None)

    start_top = jnp.full((HEADS, tok_count), -1e20, jnp.float32)
    start_total = jnp.zeros((HEADS, tok_count), jnp.float32)
    (row_top, row_total), unused = lax.scan(max_step, (start_top, start_total), key_blocks)
    log_total = row_top + jnp.log(row_total)

    def out_step(summed, portion):
        scores = masked_scores(
            query_heads, portion[0], seg_query, pos_query, portion[2], portion[3], scaling
        )
        weights_low = jnp.exp(scores - log_total[..., None]).astype(jnp.bfloat16)
        return (
            summed
            + jnp.einsum(
                "hqk,khd->qhd", weights_low, portion[1], preferred_element_type=jnp.float32
            ),
            None,
        )

    attended, unused = lax.scan(
        out_step, jnp.zeros((tok_count, HEADS, HEAD_DIM), jnp.float32), key_blocks
    )
    attended_low = attended.reshape(tok_count, width).astype(jnp.bfloat16)
    residual = (
        stream + jnp.dot(attended_low, out_full, preferred_element_type=jnp.float32) + bias_out
    )
    second_low = layer_norm(residual, gain_two, shift_two).astype(jnp.bfloat16)
    hidden = jnp.dot(second_low, up_full, preferred_element_type=jnp.float32) + bias_up
    activated = gelu_tanh(hidden).astype(jnp.bfloat16)
    output = (
        residual + jnp.dot(activated, down_full, preferred_element_type=jnp.float32) + bias_down
    )
    again = (
        lax.all_gather(qkv_weight, "dp", axis=0, tiled=True),
        lax.all_gather(out_weight, "dp", axis=0, tiled=True),
        lax.all_gather(up_weight, "dp", axis=0, tiled=True),
        lax.all_gather(down_weight, "dp", axis=0, tiled=True),
    )
    back = (
        lax.all_gather(again[0], "seq", axis=1, tiled=True),
        lax.all_gather(again[1], "seq", axis=1, tiled=True),
        lax.all_gather(again[2], "seq", axis=1, tiled=True),
        lax.all_gather(again[3], "seq", axis=1, tiled=True),
    )
    back_qkv, back_out, back_up, back_down = (back[0], back[1], back[2], back[3])
    grad_top = cotangent[0]
    grad_down_bias = jnp.sum(grad_top.astype(jnp.float32), axis=0)
    grad_act = contract_cols(grad_top, back_down)
    grad_hidden = jax.vjp(gelu_tanh, hidden)[1](grad_act)[0].astype(jnp.bfloat16)
    grad_up_bias = jnp.sum(grad_hidden.astype(jnp.float32), axis=0)
    grad_second = contract_cols(grad_hidden, back_up)
    grad_resid, grad_gain_two, grad_shift_two = jax.vjp(layer_norm, residual, gain_two, shift_two)[
        1
    ](grad_second)
    grad_resid = grad_resid + grad_top.astype(jnp.float32)
    grad_branch = grad_resid.astype(jnp.bfloat16)
    grad_out_bias = jnp.sum(grad_branch.astype(jnp.float32), axis=0)
    grad_attended = (
        contract_cols(grad_branch, back_out)
        .astype(jnp.bfloat16)
        .reshape(tok_count, HEADS, HEAD_DIM)
    )

    def delta_step(summed, portion):
        scores = masked_scores(
            query_heads, portion[0], seg_query, pos_query, portion[2], portion[3], scaling
        )
        weights_full = jnp.exp(scores - log_total[..., None])
        grad_weights = jnp.einsum(
            "qhd,khd->hqk", grad_attended, portion[1], preferred_element_type=jnp.float32
        )
        return (summed + jnp.sum(weights_full * grad_weights, axis=-1), None)

    delta, unused = lax.scan(delta_step, jnp.zeros((HEADS, tok_count), jnp.float32), key_blocks)

    def grad_step(summed, portion):
        scores = masked_scores(
            query_heads, portion[0], seg_query, pos_query, portion[2], portion[3], scaling
        )
        weights_full = jnp.exp(scores - log_total[..., None])
        grad_weights = jnp.einsum(
            "qhd,khd->hqk", grad_attended, portion[1], preferred_element_type=jnp.float32
        )
        grad_scores = (weights_full * (grad_weights - delta[..., None])).astype(jnp.bfloat16)
        summed = summed + jnp.einsum(
            "hqk,khd->qhd", grad_scores, portion[0], preferred_element_type=jnp.float32
        )
        grad_key_part = (
            jnp.einsum("hqk,qhd->khd", grad_scores, query_heads, preferred_element_type=jnp.float32)
            * scaling
        )
        grad_value_part = jnp.einsum(
            "hqk,qhd->khd",
            weights_full.astype(jnp.bfloat16),
            grad_attended,
            preferred_element_type=jnp.float32,
        )
        return (summed, (grad_key_part, grad_value_part))

    grad_query, key_parts = lax.scan(
        grad_step, jnp.zeros((tok_count, HEADS, HEAD_DIM), jnp.float32), key_blocks
    )
    grad_query = grad_query * scaling
    key_grads = (
        lax.psum_scatter(
            key_parts[0].reshape(seq_length, width), "seq", scatter_dimension=0, tiled=True
        ),
        lax.psum_scatter(
            key_parts[1].reshape(seq_length, width), "seq", scatter_dimension=0, tiled=True
        ),
    )
    grad_mixed = jnp.concatenate(
        [
            grad_query.reshape(tok_count, width).astype(jnp.bfloat16),
            key_grads[0].astype(jnp.bfloat16),
            key_grads[1].astype(jnp.bfloat16),
        ],
        axis=1,
    )
    grad_query_bias = jnp.sum(grad_mixed[:, :width].astype(jnp.float32), axis=0)
    grad_value_bias = jnp.sum(grad_mixed[:, 2 * width :].astype(jnp.float32), axis=0)
    grad_normed = contract_cols(grad_mixed, back_qkv)
    grad_stream, grad_gain_one, grad_shift_one = jax.vjp(layer_norm, stream, gain_one, shift_one)[
        1
    ](grad_normed)
    grad_input = grad_stream + grad_resid
    local_vectors = (
        grad_gain_one,
        grad_shift_one,
        grad_query_bias,
        grad_value_bias,
        grad_out_bias,
        grad_gain_two,
        grad_shift_two,
        grad_up_bias,
        grad_down_bias,
    )
    local_mats = (
        contract_rows(normed_low, grad_mixed),
        contract_rows(attended_low, grad_branch),
        contract_rows(second_low, grad_hidden),
        contract_rows(activated, grad_top),
    )
    columns = (
        lax.psum_scatter(local_mats[0], "seq", scatter_dimension=1, tiled=True),
        lax.psum_scatter(local_mats[1], "seq", scatter_dimension=1, tiled=True),
        lax.psum_scatter(local_mats[2], "seq", scatter_dimension=1, tiled=True),
        lax.psum_scatter(local_mats[3], "seq", scatter_dimension=1, tiled=True),
        lax.psum_scatter(local_vectors[0], "seq", scatter_dimension=0, tiled=True),
        lax.psum_scatter(local_vectors[1], "seq", scatter_dimension=0, tiled=True),
        lax.psum_scatter(local_vectors[2], "seq", scatter_dimension=0, tiled=True),
        lax.psum_scatter(local_vectors[3], "seq", scatter_dimension=0, tiled=True),
        lax.psum_scatter(local_vectors[4], "seq", scatter_dimension=0, tiled=True),
        lax.psum_scatter(local_vectors[5], "seq", scatter_dimension=0, tiled=True),
        lax.psum_scatter(local_vectors[6], "seq", scatter_dimension=0, tiled=True),
        lax.psum_scatter(local_vectors[7], "seq", scatter_dimension=0, tiled=True),
        lax.psum_scatter(local_vectors[8], "seq", scatter_dimension=0, tiled=True),
    )
    matrix_sums = (
        lax.psum_scatter(columns[0], "dp", scatter_dimension=0, tiled=True),
        lax.psum_scatter(columns[1], "dp", scatter_dimension=0, tiled=True),
        lax.psum_scatter(columns[2], "dp", scatter_dimension=0, tiled=True),
        lax.psum_scatter(columns[3], "dp", scatter_dimension=0, tiled=True),
    )
    vector_sums = lax.psum(
        (
            columns[4],
            columns[5],
            columns[6],
            columns[7],
            columns[8],
            columns[9],
            columns[10],
            columns[11],
            columns[12],
        ),
        "dp",
    )
    return (
        output.astype(jnp.bfloat16)[None],
        grad_input[None],
        vector_sums[0],
        vector_sums[1],
        matrix_sums[0],
        vector_sums[2],
        vector_sums[3],
        matrix_sums[1],
        vector_sums[4],
        vector_sums[5],
        vector_sums[6],
        matrix_sums[2],
        vector_sums[7],
        matrix_sums[3],
        vector_sums[8],
    )


def solution(mesh):
    placed = (
        P("dp", "seq", None),
        P("dp", "seq"),
        P("dp", "seq", None),
        P("seq"),
        P("seq"),
        P("dp", "seq"),
        P("seq"),
        P("seq"),
        P("dp", "seq"),
        P("seq"),
        P("seq"),
        P("seq"),
        P("dp", "seq"),
        P("seq"),
        P("dp", "seq"),
        P("seq"),
    )
    return jax.shard_map(
        shards,
        mesh=mesh,
        in_specs=placed,
        out_specs=(
            P("dp", "seq", None),
            P("dp", "seq", None),
            P("seq"),
            P("seq"),
            P("dp", "seq"),
            P("seq"),
            P("seq"),
            P("dp", "seq"),
            P("seq"),
            P("seq"),
            P("seq"),
            P("dp", "seq"),
            P("seq"),
            P("dp", "seq"),
            P("seq"),
        ),
        check_vma=False,
    )
```

profile of v0, /device:TPU:2, one launch (start us, length us, event | category | flops | bytes accessed | tf_op | source)
XLA Modules:
  0.0 2893.0 jit_solution(11071952138376906620)
XLA Ops:
  8.1 37.8 %all-gather.12.cloned.1.call-done = bf16[1600,600]{1,0:T(8,128)(2,1)} async-done(((bf16[400,600]{1,0:T(8,128)(2,1)}), bf16[1600,600]{1,0:T(8,128)(2,1)}) %all-gather.12.cloned.1.call-update) | async-done | bytes 1920016 | tf_op jit(solution)/shard_map/all_gather | solution.py:60
  55.5 31.6 %all-reduce.26 = (bf16[1600]{0:T(1024)(128)(2,1)S(1)}, bf16[1600]{0:T(1024)(128)(2,1)S(1)}, bf16[1600]{0:T(1024)(128)(2,1)S(1)}, bf16[1600]{0:T(1024)(128)(2,1)S...) all-reduce(bf16[1600]{0:T(1024)(128)(2,1)S(1)} %dynamic-update-slic, ...), channel_id=1, replica_groups=mesh['dp'=4,'seq'=8] {'seq'}, use_global_device_ids=true, to_apply=%add.2 | all-reduce | flops 19200 | bytes 76800
  87.7 107.9 %all-gather.14.cloned.1.call-done = bf16[1600,4800]{0,1:T(8,128)(2,1)} async-done(((bf16[1600,600]{0,1:T(8,128)(2,1)}), bf16[1600,4800]{0,1:T(8,128)(2,1)}) %all-gather.14.cloned.1.call-update) | async-done | bytes 15360016 | tf_op jit(solution)/shard_map/all_gather | solution.py:66
  195.6 10.1 fusion.91
  207.4 14.5 all_gather.77
  223.1 16.7 all-gather.22.cloned.1.call-done
  245.5 35.9 %all-gather.28.cloned.1.call-done = bf16[4,1600,200]{1,2,0:T(8,128)(2,1)} async-done(((bf16[1,1600,200]{1,2,0:T(8,128)(2,1)}), bf16[4,1600,200]{1,2,0:T(8,128)(2,1)}) %all-gather.28.cloned.1.call-update) | async-done | bytes 2560016 | tf_op jit(solution)/shard_map/all_gather | solution.py:63
  287.9 12.0 all-gather
  300.0 23.7 all-gather.16.cloned.1.call-done
  323.8 7.4 reshape.389
  333.6 30.7 %all-gather.18.cloned.1.call-done = bf16[1024,1600]{0,1:T(8,128)(2,1)} async-done(((bf16[128,1600]{0,1:T(8,128)(2,1)}), bf16[1024,1600]{0,1:T(8,128)(2,1)}) %all-gather.18.cloned.1.call-update) | async-done | bytes 3276816 | tf_op jit(solution)/shard_map/all_gather | solution.py:107
  364.3 7.4 reshape.395
  374.0 20.2 while.50
  374.3 5.6 fusion.192
  384.4 5.6 fusion.192
  394.3 9.7 while.51
  404.1 17.3 all-gather.20.cloned.1.call-done
  425.7 184.2 %all-gather.24.cloned.1.call-done = bf16[1600,6400]{0,1:T(8,128)(2,1)} async-done(((bf16[1600,800]{0,1:T(8,128)(2,1)}), bf16[1600,6400]{0,1:T(8,128)(2,1)}) %all-gather.24.cloned.1.call-update) | async-done | bytes 20480016 | tf_op jit(solution)/shard_map/all_gather | solution.py:68
  609.9 13.1 convolution_add_fusion
  623.1 168.2 %all-gather.26.cloned.1.call-done = bf16[6400,1600]{0,1:T(8,128)(2,1)} async-done(((bf16[6400,200]{0,1:T(8,128)(2,1)}), bf16[6400,1600]{0,1:T(8,128)(2,1)}) %all-gather.26.cloned.1.call-update) | async-done | bytes 20480016 | tf_op jit(solution)/shard_map/all_gather | solution.py:69
  791.2 13.9 convert_reduce_fusion
  805.1 15.1 multiply_reduce_fusion
  829.9 13.5 while.52
  843.4 285.3 %while.53 = (s32[]{:T(128)}, f32[128,25,64]{0,2,1:T(8,128)}, f32[2,512,25,64]{1,0,3,2:T(2,128)}, f32[2,512,25,64]{1,0,3,2:T(2,128)}, bf16[2,512,25,64]{1,3,2,0:T...) while((s32[]{:T(128)}, f32[128,25,64]{0,2,1:T(8,128)}, ...), condition=%wide.region_16.17_spmd.clone, body=%wide.region_15.16_spmd.clone.sunk | while | flops 1066385536 | bytes 96914648 | solution.py:231
  846.6 5.6 fusion.216
  861.0 58.4 %dynamic_update_slice.11 = f32[2,512,25,64]{1,0,3,2:T(2,128)} dynamic-update-slice(f32[2,512,25,64]{1,0,3,2:T(2,128)} %get-tuple-element.1213, f32[1,512,25,64]{1,0,3,2:T(1,128)S(1)} %copy.139, s32[]{:T(128)S(6)} %copy.177, s32[]{:T(128)} %constant.93.clone.1..sunk.3, s32[]{:T(128)} %constant.93.clone.1..sunk.3, s32[]{:T(128)} %constant.93.clone.1..sunk.3) | dynamic-update-slice | bytes 6553604 | tf_op jit(solution)/shard_map/while/body/jit(dynamic_update_index_in_dim)/dynamic_update_slice | solution.py:231
  927.6 58.5 %dynamic_update_slice.12 = f32[2,512,25,64]{1,0,3,2:T(2,128)} dynamic-update-slice(f32[2,512,25,64]{1,0,3,2:T(2,128)} %get-tuple-element.1214, f32[1,512,25,64]{1,0,3,2:T(1,128)S(1)} %copy.140, s32[]{:T(128)S(6)} %copy.177, s32[]{:T(128)} %constant.93.clone.1..sunk.3, s32[]{:T(128)} %constant.93.clone.1..sunk.3, s32[]{:T(128)} %constant.93.clone.1..sunk.3) | dynamic-update-slice | bytes 6553604 | tf_op jit(solution)/shard_map/while/body/jit(dynamic_update_index_in_dim)/dynamic_update_slice | solution.py:231
  1003.4 58.4 %dynamic_update_slice.11 = f32[2,512,25,64]{1,0,3,2:T(2,128)} dynamic-update-slice(f32[2,512,25,64]{1,0,3,2:T(2,128)} %get-tuple-element.1213, f32[1,512,25,64]{1,0,3,2:T(1,128)S(1)} %copy.139, s32[]{:T(128)S(6)} %copy.177, s32[]{:T(128)} %constant.93.clone.1..sunk.3, s32[]{:T(128)} %constant.93.clone.1..sunk.3, s32[]{:T(128)} %constant.93.clone.1..sunk.3) | dynamic-update-slice | bytes 6553604 | tf_op jit(solution)/shard_map/while/body/jit(dynamic_update_index_in_dim)/dynamic_update_slice | solution.py:231
  1070.0 58.5 %dynamic_update_slice.12 = f32[2,512,25,64]{1,0,3,2:T(2,128)} dynamic-update-slice(f32[2,512,25,64]{1,0,3,2:T(2,128)} %get-tuple-element.1214, f32[1,512,25,64]{1,0,3,2:T(1,128)S(1)} %copy.140, s32[]{:T(128)S(6)} %copy.177, s32[]{:T(128)} %constant.93.clone.1..sunk.3, s32[]{:T(128)} %constant.93.clone.1..sunk.3, s32[]{:T(128)} %constant.93.clone.1..sunk.3) | dynamic-update-slice | bytes 6553604 | tf_op jit(solution)/shard_map/while/body/jit(dynamic_update_index_in_dim)/dynamic_update_slice | solution.py:231
  1128.6 7.2 copy.136
  1135.9 7.2 copy.135
  1144.6 61.8 %reduce-scatter.23.cloned.1.call-done = f32[128,1600]{0,1:T(8,128)} async-done(((f32[1024,1600]{0,1:T(8,128)}), f32[128,1600]{0,1:T(8,128)}) %reduce-scatter.23.cloned.1.call-update) | async-done | bytes 819216 | tf_op jit(solution)/shard_map/reduce_scatter | solution.py:239
  1208.5 71.0 %reduce-scatter.21.cloned.1.call-done = f32[128,1600]{0,1:T(8,128)} async-done(((f32[1024,1600]{0,1:T(8,128)}), f32[128,1600]{0,1:T(8,128)}) %reduce-scatter.21.cloned.1.call-update) | async-done | bytes 819216 | tf_op jit(solution)/shard_map/reduce_scatter | solution.py:236
  1280.7 15.4 fusion.116
  1297.8 17.2 fusion.131
  1316.0 18.3 fusion.118
  1342.0 11.6 fusion.132
  1354.9 251.3 %reduce-scatter.31.cloned.1.call-done = f32[1600,600]{0,1:T(8,128)} async-done(((f32[1600,4800]{0,1:T(8,128)}), f32[1600,600]{0,1:T(8,128)}) %reduce-scatter.31.cloned.1.call-update) | async-done | bytes 3840016
  1606.1 412.3 %reduce-scatter.25.cloned.1.call-done = f32[1600,800]{0,1:T(8,128)} async-done(((f32[1600,6400]{0,1:T(8,128)}), f32[1600,800]{0,1:T(8,128)}) %reduce-scatter.25.cloned.1.call-update) | async-done | bytes 5120016 | tf_op jit(solution)/shard_map/reduce_scatter | solution.py:278
  2018.5 396.9 %reduce-scatter.35.cloned.1.call-done = f32[6400,200]{0,1:T(8,128)} async-done(((f32[6400,1600]{0,1:T(8,128)}), f32[6400,200]{0,1:T(8,128)}) %reduce-scatter.35.cloned.1.call-update) | async-done | bytes 5120016
  2415.4 6.7 copy.112
  2422.2 105.0 %reduce-scatter.33.cloned.1.call-done = f32[1600,200]{0,1:T(8,128)} async-done(((f32[1600,1600]{0,1:T(8,128)}), f32[1600,200]{0,1:T(8,128)}) %reduce-scatter.33.cloned.1.call-update) | async-done | bytes 1280016
  2532.9 11.5 fusion.102
  2545.7 37.2 %all-reduce.30.cloned.1.call-done = (f32[1600]{0:T(1024)}, f32[1600]{0:T(1024)}, f32[1600]{0:T(1024)}, f32[1600]{0:T(1024)}, f32[1600]{0:T(1024)}, /*index=5*/f3...) async-done(((f32[1600]{0:T(1024)}, f32[1600]{0:T(1024)}, f32[1600]{0:T(1024)}, f32[1600]{0:T(1024)}, f32[1600]{0:T(1024)}, /*index=5*/f32[1600]{0:T(1024)}, ...) | async-done | bytes 76816
  2589.8 15.4 all-reduce.24
  2605.2 170.3 %all-reduce.32.cloned.1.call-done = (f32[1600,600]{0,1:T(8,128)}, f32[1600,800]{0,1:T(8,128)}) async-done(((f32[1600,600]{0,1:T(8,128)}, f32[1600,800]{0,1:T(8,128)}), (f32[1600,600]{0,1:T(8,128)}, f32[1600,800]{0,1:T(8,128)})) %all-reduce.32.cloned.1.call-update) | async-done | bytes 8960016
  2782.3 68.6 %reduce-scatter.29.cloned.1.call-done = f32[1600,200]{1,0:T(8,128)} async-done(((f32[6400,200]{1,0:T(8,128)}), f32[1600,200]{1,0:T(8,128)}) %reduce-scatter.29.cloned.1.call-update) | async-done | bytes 1280016
  2853.8 32.2 %reduce-scatter.27.cloned.1.call-done = f32[400,200]{1,0:T(8,128)} async-done(((f32[1600,200]{1,0:T(8,128)}), f32[400,200]{1,0:T(8,128)}) %reduce-scatter.27.cloned.1.call-update) | async-done | bytes 320016
  (290 shorter events, 158.4 us)
Async XLA Ops:
  7.2 38.7 %all-gather.12.cloned.1.call-start = ((), (), s32[]{:S(2)}) async-start(), calls=%async_computation.8 | async-start | bytes 2560000 | tf_op jit(solution)/shard_map/all_gather | solution.py:60
  7.9 45.3 %copy-start.46 = (bf16[200]{0:T(256)(128)(2,1)S(1)}, bf16[200]{0:T(256)(128)(2,1)}, u32[]{:S(2)}) copy-start(bf16[200]{0:T(256)(128)(2,1)} %param.30) | copy-start | bytes 1204
  7.9 45.5 %copy-start.47 = (bf16[200]{0:T(256)(128)(2,1)S(1)}, bf16[200]{0:T(256)(128)(2,1)}, u32[]{:S(2)}) copy-start(bf16[200]{0:T(256)(128)(2,1)} %param.31) | copy-start | bytes 1204
  8.0 45.8 %copy-start.48 = (bf16[200]{0:T(256)(128)(2,1)S(1)}, bf16[200]{0:T(256)(128)(2,1)}, u32[]{:S(2)}) copy-start(bf16[200]{0:T(256)(128)(2,1)} %param.28) | copy-start | bytes 1204
  8.0 46.0 %copy-start.49 = (bf16[200]{0:T(256)(128)(2,1)S(1)}, bf16[200]{0:T(256)(128)(2,1)}, u32[]{:S(2)}) copy-start(bf16[200]{0:T(256)(128)(2,1)} %param.27) | copy-start | bytes 1204
  8.0 46.3 %copy-start.50 = (bf16[200]{0:T(256)(128)(2,1)S(1)}, bf16[200]{0:T(256)(128)(2,1)}, u32[]{:S(2)}) copy-start(bf16[200]{0:T(256)(128)(2,1)} %param.33) | copy-start | bytes 1204
  8.0 46.5 %copy-start.51 = (bf16[200]{0:T(256)(128)(2,1)S(1)}, bf16[200]{0:T(256)(128)(2,1)}, u32[]{:S(2)}) copy-start(bf16[200]{0:T(256)(128)(2,1)} %param.39) | copy-start | bytes 1204
  8.0 46.8 %copy-start.52 = (bf16[200]{0:T(256)(128)(2,1)S(1)}, bf16[200]{0:T(256)(128)(2,1)}, u32[]{:S(2)}) copy-start(bf16[200]{0:T(256)(128)(2,1)} %param.35) | copy-start | bytes 1204
  8.0 47.0 %copy-start.53 = (bf16[200]{0:T(256)(128)(2,1)S(1)}, bf16[200]{0:T(256)(128)(2,1)}, u32[]{:S(2)}) copy-start(bf16[200]{0:T(256)(128)(2,1)} %param.34) | copy-start | bytes 1204
  8.0 47.2 %copy-start.43 = (bf16[800]{0:T(1024)(128)(2,1)S(1)}, bf16[800]{0:T(1024)(128)(2,1)}, u32[]{:S(2)}) copy-start(bf16[800]{0:T(1024)(128)(2,1)} %param.37) | copy-start | bytes 4804
  8.0 79.1 %copy-start.4 = (bf16[1,128,1600]{1,2,0:T(8,128)(2,1)S(1)}, bf16[1,128,1600]{1,2,0:T(8,128)(2,1)}, u32[]{:S(2)}) copy-start(bf16[1,128,1600]{1,2,0:T(8,128)(2,1)} %param.24) | copy-start | bytes 1228804
  8.0 187.5 %all-gather.14.cloned.1.call-start = ((), (), s32[]{:S(2)}) async-start(), calls=%async_computation.9 | async-start | bytes 17971200 | tf_op jit(solution)/shard_map/all_gather | solution.py:66
  49.9 189.9 %all-gather.22.cloned.1.call-start = ((), (), s32[]{:S(2)}) async-start(), calls=%async_computation.13 | async-start | bytes 3584000 | tf_op jit(solution)/shard_map/all_gather | solution.py:62
  50.7 230.7 %all-gather.28.cloned.1.call-start = ((), (), s32[]{:S(2)}) async-start(), calls=%async_computation.19 | async-start | bytes 3328000 | tf_op jit(solution)/shard_map/all_gather | solution.py:63
  51.3 272.5 %all-gather.16.cloned.1.call-start = ((), (), s32[]{:S(2)}) async-start(), calls=%async_computation.10 | async-start | bytes 3686400 | tf_op jit(solution)/shard_map/all_gather | solution.py:108
  87.1 118.6 %copy-start.29 = (f32[1600]{0:T(1024)}, f32[1600]{0:T(1024)S(1)}, u32[]{:S(2)}) copy-start(f32[1600]{0:T(1024)S(1)} %convert_element_type.112) | copy-start | bytes 19204
  87.1 118.6 %copy-start.25 = (f32[1600]{0:T(1024)}, f32[1600]{0:T(1024)S(1)}, u32[]{:S(2)}) copy-start(f32[1600]{0:T(1024)S(1)} %convert_element_type.111) | copy-start | bytes 19204
  87.4 118.3 %copy-start.35 = (f32[128]{0:T(128)}, f32[128]{0:T(128)S(1)}, u32[]{:S(2)}) copy-start(f32[128]{0:T(128)S(1)} %broadcast_multiply_fusion.1) | copy-start | bytes 1540
  87.6 118.0 %copy-start.44 = (f32[128]{0:T(128)}, f32[128]{0:T(128)S(1)}, u32[]{:S(2)}) copy-start(f32[128]{0:T(128)S(1)} %fusion.113) | copy-start | bytes 1540
  87.6 118.0 %copy-start.37 = (f32[128]{0:T(128)}, f32[128]{0:T(128)S(1)}, u32[]{:S(2)}) copy-start(f32[128]{0:T(128)S(1)} %fusion.125) | copy-start | bytes 1540
  206.8 157.5 %all-gather.18.cloned.1.call-start = ((), (), s32[]{:S(2)}) async-start(), calls=%async_computation.11 | async-start | bytes 3686400 | tf_op jit(solution)/shard_map/all_gather | solution.py:107
  207.4 214.0 %all-gather.20.cloned.1.call-start = ((), (), s32[]{:S(2)}) async-start(), calls=%async_computation.12 | async-start | bytes 5990400 | tf_op jit(solution)/shard_map/all_gather | solution.py:67
  223.1 386.9 %all-gather.24.cloned.1.call-start = ((), (), s32[]{:S(2)}) async-start(), calls=%async_computation.14 | async-start | bytes 23961600 | tf_op jit(solution)/shard_map/all_gather | solution.py:68
  245.0 546.2 %all-gather.26.cloned.1.call-start = ((), (), s32[]{:S(2)}) async-start(), calls=%async_computation.15 | async-start | bytes 23040000 | tf_op jit(solution)/shard_map/all_gather | solution.py:69
  287.8 918.6 %reduce-scatter.23.cloned.1.call-start = ((), (), s32[]{:S(2)}) async-start(), calls=%async_computation.17 | async-start | bytes 7372800 | tf_op jit(solution)/shard_map/reduce_scatter | solution.py:239
  300.0 310.0 %copy-start.23 = (f32[1600]{0:T(1024)}, f32[1600]{0:T(1024)S(1)}, u32[]{:S(2)}) copy-start(f32[1600]{0:T(1024)S(1)} %convert_element_type.123) | copy-start | bytes 19204
  300.0 520.2 %copy-start.21 = (f32[1600]{0:T(1024)}, f32[1600]{0:T(1024)S(1)}, u32[]{:S(2)}) copy-start(f32[1600]{0:T(1024)S(1)} %convert_element_type.122) | copy-start | bytes 19204
  425.5 394.8 %copy-start.2 = (f32[128,1600]{0,1:T(8,128)}, f32[128,1600]{0,1:T(8,128)S(1)}, u32[]{:S(2)}) copy-start(f32[128,1600]{0,1:T(8,128)S(1)} %get-tuple-element.794) | copy-start | bytes 2457604
  425.5 394.8 %copy-start.31 = (f32[128]{0:T(128)}, f32[128]{0:T(128)S(1)}, u32[]{:S(2)}) copy-start(f32[128]{0:T(128)S(1)} %broadcast_multiply_fusion) | copy-start | bytes 1540
  425.7 394.5 %copy-start.33 = (f32[128]{0:T(128)}, f32[128]{0:T(128)S(1)}, u32[]{:S(2)}) copy-start(f32[128]{0:T(128)S(1)} %fusion.126) | copy-start | bytes 1540
  425.7 365.5 %copy-start.11 = (bf16[1,128,1600]{1,2,0:T(8,128)(2,1)S(1)}, bf16[1,128,1600]{1,2,0:T(8,128)(2,1)}, u32[]{:S(2)}) copy-start(bf16[1,128,1600]{1,2,0:T(8,128)(2,1)} %param.26) | copy-start | bytes 1228804
  1135.9 143.6 %reduce-scatter.21.cloned.1.call-start = ((), (), s32[]{:S(2)}) async-start(), calls=%async_computation.16 | async-start | bytes 7372800 | tf_op jit(solution)/shard_map/reduce_scatter | solution.py:236
  1143.2 137.4 %copy-start.6 = (bf16[1,128,1600]{1,2,0:T(8,128)(2,1)S(1)}, bf16[1,128,1600]{1,2,0:T(8,128)(2,1)}, u32[]{:S(2)}) copy-start(bf16[1,128,1600]{1,2,0:T(8,128)(2,1)} %param.24) | copy-start | bytes 1228804
  1143.2 137.4 %copy-start.26 = (f32[1600]{0:T(1024)S(1)}, f32[1600]{0:T(1024)}, u32[]{:S(2)}) copy-start(f32[1600]{0:T(1024)} %copy-done.25) | copy-start | bytes 19204
  1143.2 137.4 %copy-start.30 = (f32[1600]{0:T(1024)S(1)}, f32[1600]{0:T(1024)}, u32[]{:S(2)}) copy-start(f32[1600]{0:T(1024)} %copy-done.29) | copy-start | bytes 19204
  1143.2 137.4 %copy-start.36 = (f32[128]{0:T(128)S(1)}, f32[128]{0:T(128)}, u32[]{:S(2)}) copy-start(f32[128]{0:T(128)} %copy-done.35) | copy-start | bytes 1540
  1143.2 137.4 %copy-start.38 = (f32[128]{0:T(128)S(1)}, f32[128]{0:T(128)}, u32[]{:S(2)}) copy-start(f32[128]{0:T(128)} %copy-done.37) | copy-start | bytes 1540
  1143.2 462.9 %reduce-scatter.31.cloned.1.call-start = ((), (), s32[]{:S(2)}) async-start(), calls=%async_computation.22 | async-start | bytes 35942400
  1208.5 87.6 %copy-start.17 = (bf16[128,1600]{0,1:T(8,128)(2,1)}, bf16[128,1600]{0,1:T(8,128)(2,1)S(1)}, u32[]{:S(2)}) copy-start(bf16[128,1600]{0,1:T(8,128)(2,1)S(1)} %get-tuple-element.772) | copy-start | bytes 1228804
  1296.2 722.3 %reduce-scatter.25.cloned.1.call-start = ((), (), s32[]{:S(2)}) async-start(), calls=%async_computation.18 | async-start | bytes 47923200 | tf_op jit(solution)/shard_map/reduce_scatter | solution.py:278
  1315.1 1100.4 %reduce-scatter.35.cloned.1.call-start = ((), (), s32[]{:S(2)}) async-start(), calls=%async_computation.24 | async-start | bytes 46080000
  1334.3 1192.9 %reduce-scatter.33.cloned.1.call-start = ((), (), s32[]{:S(2)}) async-start(), calls=%async_computation.23 | async-start | bytes 11980800
  1341.0 1241.9 %all-reduce.30.cloned.1.call-start = ((), (), s32[]{:S(2)}) async-start(), calls=%async_computation.25 | async-start | bytes 188416
  1354.8 1420.7 %all-reduce.32.cloned.1.call-start = ((), (), s32[]{:S(2)}) async-start(), calls=%async_computation.26 | async-start | bytes 18636800
  2018.5 832.4 %reduce-scatter.29.cloned.1.call-start = ((), (), s32[]{:S(2)}) async-start(), calls=%async_computation.21 | async-start | bytes 8192000
  2422.2 108.1 %copy-start.39 = (bf16[1600]{0:T(1024)(128)(2,1)S(1)}, bf16[1600]{0:T(1024)(128)(2,1)}, u32[]{:S(2)}) copy-start(bf16[1600]{0:T(1024)(128)(2,1)} %get-tuple-element.765) | copy-start | bytes 9604
  2422.2 109.4 %copy-start.54 = (u32[32]{0:T(128)S(1)}, u32[32]{0:T(128)}, u32[]{:S(2)}) copy-start(u32[32]{0:T(128)} %constant.180) | copy-start | bytes 388
  2422.2 463.8 %reduce-scatter.27.cloned.1.call-start = ((), (), s32[]{:S(2)}) async-start(), calls=%async_computation.20 | async-start | bytes 2048000
  (27 other events, 219.1 us)
Sparse Core Ops, SparseCore 0:
  9.8 35.9 all-gather.11
  50.1 145.4 all-gather.13
  197.4 42.3 all-gather.21
  241.5 39.8 all-gather.27
  283.4 40.2 all-gather.15
  325.8 38.4 all-gather.17
  366.5 54.8 all-gather.19
  423.0 186.8 all-gather.23
  611.6 179.6 all-gather.25
  1136.0 70.3 reduce-scatter.22
  1208.7 70.6 reduce-scatter.20
  1296.3 309.7 reduce-scatter.30
  1608.5 409.9 reduce-scatter.24
  2020.7 394.6 reduce-scatter.34
  2417.6 109.5 reduce-scatter.32
  2530.8 52.0 all-reduce.29
  2586.5 188.9 all-reduce.31
  2778.4 72.3 reduce-scatter.28
  2854.4 31.5 reduce-scatter.26
where the time goes:
time: 2920 us; the launch traced here: 2890 us
  waiting for transfers between devices  2230 us (76%)
  local copies, waits for them, and re-layouts  337 us (12%)
  matrix products  211 us (7%)
  blocking collectives  73.5 us (3%)
    unnamed x26, waiting for transfers between devices  1060 us
    reduce_scatter x1, waiting for transfers between devices, shards(): lax.psum_scatter(local_mats[2], 'seq', scatter_dimension=1, tiled=True)  412 us
    dynamic_update_slice x8, local copies, waits for them, and re-layouts, shards(): lax.scan(grad_step, jnp.zeros((tok_count, HEADS, HEAD_DIM), jnp.float32),...  248 us
    all_gather x1, waiting for transfers between devices, shards(): lax.all_gather(rows[2], 'seq', axis=1, tiled=True)  184 us
    all_gather x1, waiting for transfers between devices, shards(): lax.all_gather(rows[3], 'seq', axis=1, tiled=True)  168 us
    all_gather x1, waiting for transfers between devices, shards(): lax.all_gather(rows[0], 'seq', axis=1, tiled=True)  108 us
    reduce_scatter x1, waiting for transfers between devices, shards(): lax.psum_scatter(key_parts[0].reshape(seq_length, width), 'seq', scatter_...  71 us
    reduce_scatter x1, waiting for transfers between devices, shards(): lax.psum_scatter(key_parts[1].reshape(seq_length, width), 'seq', scatter_...  61.8 us
  transfers between devices with their start and end apart: 19, of which 19 were waited for; matrix products, arithmetic and copies ran while one was open for 7% of the time, Pallas kernels for 0%

commit v1 on v0

v1 whole, which is shorter than its diff:
```python
import functools

import jax
import jax.numpy as jnp
from jax import lax
from jax.experimental import pallas as pl
from jax.experimental.pallas import tpu as pltpu
from jax.sharding import PartitionSpec as P

HEADS = 25
HEAD_DIM = 64
CORES = 2
MESH = pl.DeviceIdType.MESH
F32 = jnp.float32
BF16 = jnp.bfloat16
ANY = pl.BlockSpec(memory_space=pl.ANY)
VMEM = pl.BlockSpec(memory_space=pltpu.VMEM)
VMEM_LIMIT = 60 * 1024 * 1024


def layer_norm(values, gain, shift):
    center = values - jnp.mean(values, axis=-1, keepdims=True)
    spread = jnp.mean(center * center, axis=-1, keepdims=True)
    return center * lax.rsqrt(spread + 1e-05) * gain + shift


def gelu_tanh(values):
    return jax.nn.gelu(values, approximate=True)


def dot(left, right, dims):
    return lax.dot_general(left, right, (dims, ((), ())), preferred_element_type=F32)


NN = ((1,), (0,))
NT = ((1,), (1,))
TN = ((0,), (0,))


class Plan:
    def __init__(self, nd, nq, tokens, width, ff):
        self.nd, self.nq, self.nc = nd, nq, nq // CORES
        self.tl, self.length, self.width, self.ff = tokens, tokens * nq, width, ff
        self.ratio = nq // nd
        self.slots = -(-HEADS // nq)
        self.kd = width // nd
        self.cq = width // nq
        self.fq = ff // nq
        self.gq = HEAD_DIM // nq
        self.go = HEAD_DIM // nd
        self.groups_q = 3 * self.slots * nq
        self.groups_o = self.slots * nd
        self.hw = self.slots * HEAD_DIM

    def owner(self, head):
        return (head * self.nq) // HEADS

    def first(self, q):
        return (HEADS * q + self.nq - 1) // self.nq

    def count(self, q):
        return self.first(q + 1) - self.first(q)


def here():
    return lax.axis_index("dp"), lax.axis_index("seq")


def remote(src, dst, send, recv, d, q):
    return pltpu.make_async_remote_copy(
        src_ref=src, dst_ref=dst, send_sem=send, recv_sem=recv, device_id=(d, q), device_id_type=MESH
    )


def local(src, dst, sem):
    return pltpu.make_async_copy(src, dst, sem)


def wait_for(ref, sem):
    pltpu.make_async_copy(ref, ref, sem).wait()


def signal(sem, d, q):
    pl.semaphore_signal(sem, inc=1, device_id=(d, q), device_id_type=MESH)


def greet_all(plan):
    d, q = here()
    me = d * plan.nq + q
    barrier = pltpu.get_barrier_semaphore()
    total = plan.nd * plan.nq

    def one(k, carry):
        other = lax.rem(me + k, total)
        signal(barrier, other // plan.nq, lax.rem(other, plan.nq))
        return carry

    lax.fori_loop(1, total, one, 0)
    pl.semaphore_wait(barrier, total - 1)


def greet_chain(plan):
    d, q = here()
    chip, core = q // CORES, lax.rem(q, CORES)
    barrier = pltpu.get_barrier_semaphore()
    signal(barrier, d, q + 1 - 2 * core)

    @pl.when(chip < plan.nc - 1)
    def _():
        signal(barrier, d, q + CORES)

    @pl.when(chip > 0)
    def _():
        signal(barrier, d, q - CORES)

    pl.semaphore_wait(barrier, 1 + jnp.minimum(chip, 1) + jnp.minimum(plan.nc - 1 - chip, 1))


class Gather:
    def __init__(self, plan, own, buf, send, recv, loc):
        self.plan, self.own, self.buf, self.send, self.recv, self.loc = plan, own, buf, send, recv, loc
        self.d, self.q = here()
        self.chip, self.core = self.q // CORES, lax.rem(self.q, CORES)

    @staticmethod
    def sems(plan):
        return [
            pltpu.SemaphoreType.DMA((3, plan.nc)),
            pltpu.SemaphoreType.DMA((plan.nq,)),
            pltpu.SemaphoreType.DMA,
        ]

    def push(self, src, origin, way):
        slot = origin * CORES + self.core
        to = (self.q + CORES, self.q - CORES, self.q + 1 - 2 * self.core)[way]
        return remote(
            src, self.buf.at[slot], self.send.at[way, origin], self.recv.at[slot], self.d, to
        )

    def start(self):
        @pl.when(self.chip < self.plan.nc - 1)
        def _():
            self.push(self.own, self.chip, 0).start()

        @pl.when(self.chip > 0)
        def _():
            self.push(self.own, self.chip, 1).start()

        self.push(self.own, self.chip, 2).start()
        local(self.own, self.buf.at[self.q], self.loc).start()

    def step(self, s):
        nc = self.plan.nc

        def arrive(origin, way):
            slot = origin * CORES + self.core
            wait_for(self.buf.at[slot], self.recv.at[slot])

            @pl.when((self.chip < nc - 1) if way == 0 else (self.chip > 0))
            def _():
                self.push(self.buf.at[slot], origin, way).start()

            self.push(self.buf.at[slot], origin, 2).start()

        @pl.when(self.chip >= s)
        def _():
            arrive(self.chip - s, 0)

        @pl.when(self.chip + s < nc)
        def _():
            arrive(self.chip + s, 1)

    def finish(self):
        nc = self.plan.nc
        wait_for(self.own, self.loc)
        for o in range(nc):
            slot = o * CORES + 1 - self.core
            wait_for(self.buf.at[slot], self.recv.at[slot])
        for o in range(nc):
            wait_for(self.own, self.send.at[2, o])

            @pl.when((o <= self.chip) & (self.chip < nc - 1))
            def _():
                wait_for(self.own, self.send.at[0, o])

            @pl.when((o >= self.chip) & (self.chip > 0))
            def _():
                wait_for(self.own, self.send.at[1, o])


class Scatter:
    def __init__(self, plan, part, swap, flow, run, sems):
        self.plan, self.part, self.swap, self.flow, self.run = plan, part, swap, flow, run
        self.s_swap, self.r_swap, self.s_flow, self.r_flow = sems
        self.d, self.q = here()
        self.chip, self.core = self.q // CORES, lax.rem(self.q, CORES)

    @staticmethod
    def scratch(plan):
        block = (plan.tl, plan.width)
        return [
            pltpu.VMEM((plan.nc, *block), BF16),
            pltpu.VMEM((2, plan.nc, *block), BF16),
            pltpu.VMEM((2, plan.nc, *block), BF16),
            pltpu.SemaphoreType.DMA((plan.nc,)),
            pltpu.SemaphoreType.DMA((plan.nc,)),
            pltpu.SemaphoreType.DMA((2, plan.nc)),
            pltpu.SemaphoreType.DMA((2, plan.nc)),
        ]

    def order(self):
        nc = self.plan.nc
        seen = []
        for k in range(nc):
            for o in (nc - 1 - k, k):
                if o not in seen:
                    seen.append(o)
        return seen

    def swap_out(self, o):
        remote(
            self.part.at[o * CORES + 1 - self.core],
            self.swap.at[o],
            self.s_swap.at[o],
            self.r_swap.at[o],
            self.d,
            self.q + 1 - 2 * self.core,
        ).start()

    def pair_sum(self, o):
        return self.part[o * CORES + self.core].astype(F32) + self.swap[o].astype(F32)

    def forward(self, o, way):
        plan, chip = self.plan, self.chip
        active = (chip < o) if way == 0 else (chip > o)
        inner = (chip > 0) if way == 0 else (chip < plan.nc - 1)
        to = self.q + CORES if way == 0 else self.q - CORES

        @pl.when(active)
        def _():
            self.run[way, o] = self.pair_sum(o).astype(BF16)

            @pl.when(inner)
            def _():
                wait_for(self.flow.at[way, o], self.r_flow.at[way, o])
                self.run[way, o] = (self.pair_sum(o) + self.flow[way, o].astype(F32)).astype(BF16)

            remote(
                self.run.at[way, o],
                self.flow.at[way, o],
                self.s_flow.at[way, o],
                self.r_flow.at[way, o],
                self.d,
                to,
            ).start()

    def start(self):
        for o in self.order():
            self.swap_out(o)

    def flows(self):
        nc = self.plan.nc
        for k in range(nc - 1):
            for o in sorted({nc - 1 - k, k}):
                pass
        waited = set()
        for k in range(nc):
            for o, way in ((nc - 1 - k, 0), (k, 1)):
                if o not in waited:
                    wait_for(self.swap.at[o], self.r_swap.at[o])
                    waited.add(o)
                self.forward(o, way)

    def finish(self, out):
        plan, nc, chip = self.plan, self.plan.nc, self.chip
        out[...] = self.pair_sum(chip)

        @pl.when(chip > 0)
        def _():
            wait_for(self.flow.at[0, chip], self.r_flow.at[0, chip])
            out[...] += self.flow[0, chip].astype(F32)

        @pl.when(chip < nc - 1)
        def _():
            wait_for(self.flow.at[1, chip], self.r_flow.at[1, chip])
            out[...] += self.flow[1, chip].astype(F32)

        for o in range(nc):
            wait_for(self.swap.at[o], self.s_swap.at[o])

            @pl.when(chip < o)
            def _():
                wait_for(self.run.at[0, o], self.s_flow.at[0, o])

            @pl.when(chip > o)
            def _():
                wait_for(self.run.at[1, o], self.s_flow.at[1, o])


class Spread:
    def __init__(self, plan, axis, buf, send, recv):
        self.axis, self.buf, self.send, self.recv = axis, buf, send, recv
        self.d, self.q = here()
        self.n = plan.nd if axis == "dp" else plan.nq
        self.me = self.d if axis == "dp" else self.q

    def other(self, k):
        return lax.rem(self.me + k, self.n)

    def place(self, i):
        return (i, self.q) if self.axis == "dp" else (self.d, i)

    def start(self, block_of):
        for k in range(1, self.n):
            to = self.other(k)
            remote(
                block_of(to), self.buf.at[self.me], self.send.at[k], self.recv.at[self.me], *self.place(to)
            ).start()

    def wait(self):
        for k in range(1, self.n):
            i = self.other(k)
            wait_for(self.buf.at[i], self.recv.at[i])

    def wait_sent(self):
        for k in range(1, self.n):
            wait_for(self.buf.at[self.me], self.send.at[k])


def dma(*shape):
    return pltpu.SemaphoreType.DMA(shape)


def move(src, dst, send, recv, d, q, mine):
    @pl.when(jnp.logical_not(mine))
    def _():
        remote(src, dst, send, recv, d, q).start()

    @pl.when(mine)
    def _():
        local(src, dst, recv).start()


def start_kernel(plan, *refs):
    (x_own, c_own, vec_own, seg_own, wq_own, wo_own, wu_own, wd_own) = refs[:8]
    (gx, gc, gv, gs, wq, wo, wu, wd) = refs[8:16]
    (zq, zo, *sem) = refs[16:]
    d, q = here()
    nd, nq, r = plan.nd, plan.nq, plan.ratio
    it = iter(sem)
    ag_x = Gather(plan, x_own, gx, next(it), next(it), next(it))
    ag_c = Gather(plan, c_own, gc, next(it), next(it), next(it))
    loc = next(it)
    sp_v = Spread(plan, "seq", gv, next(it), next(it))
    sp_s = Spread(plan, "seq", gs, next(it), next(it))
    q_send, q_recv = next(it), next(it)
    sp_q = Spread(plan, "dp", wq, next(it), next(it))
    o_send, o_recv = next(it), next(it)
    sp_o = Spread(plan, "dp", wo, next(it), next(it))
    d_send, d_recv = next(it), next(it)
    sp_d = Spread(plan, "dp", wd, next(it), next(it))
    sp_u = Spread(plan, "dp", wu, next(it), next(it))

    zq[...] = jnp.zeros_like(zq)
    zo[...] = jnp.zeros_like(zo)
    fills = [
        local(zq, wq.at[d, pl.ds((t * plan.slots + plan.slots - 1) * nq, nq)], loc.at[t])
        for t in range(3)
    ]
    fills += [
        local(zo, wo.at[d, s, pl.ds((plan.slots - 1) * nd, nd)], loc.at[3 + s]) for s in range(r)
    ]
    for fill in fills:
        fill.start()
    for fill in fills:
        fill.wait()
    greet_all(plan)

    ag_x.start()
    local(vec_own, gv.at[q], loc.at[0]).start()
    local(seg_own, gs.at[q], loc.at[1]).start()
    sp_v.start(lambda to: vec_own)
    sp_s.start(lambda to: seg_own)

    per_third = HEADS * nq
    per_dev = 3 * HEADS

    def qkv_group(j, carry):
        g = q * per_dev + j
        third = g // per_third
        rest = g - third * per_third
        head = rest // nq
        piece = rest - head * nq
        to = plan.owner(head)
        row = (third * plan.slots + head - plan.first(to)) * nq + piece
        move(wq_own.at[j], wq.at[d, row], q_send.at[j], q_recv, d, to, to == q)
        return carry

    lax.fori_loop(0, per_dev, qkv_group, 0)

    sp_u.start(lambda to: wu_own)
    local(wu_own, wu.at[d], loc.at[2]).start()

    for s in range(r):
        to_d, to_q = q // r, d * r + s
        mine = (to_d == d) & (to_q == q)
        move(
            wd_own.at[s],
            wd.at[to_d, lax.rem(q, r)],
            d_send.at[s],
            d_recv.at[lax.rem(q, r)],
            to_d,
            to_q,
            mine,
        )

    def out_group(j, carry):
        g = d * HEADS + j
        head = g // nd
        piece = g - head * nd
        to = plan.owner(head)
        row = (head - plan.first(to)) * nd + piece
        to_d = q // r
        mine = (to_d == d) & (to == q)
        move(wo_own.at[j], wo.at[to_d, lax.rem(q, r), row], o_send.at[j], o_recv, to_d, to, mine)
        return carry

    lax.fori_loop(0, HEADS, out_group, 0)
    ag_c.start()

    many = plan.count(q) == plan.slots
    few = jnp.logical_not(many)
    for cond, n in ((many, plan.slots), (few, plan.slots - 1)):

        @pl.when(cond)
        def _():
            wait_for(wq.at[0, pl.ds(0, 3 * n * nq)], q_recv)

    sp_q.start(lambda to: wq.at[d])
    ag_x.step(1)
    for cond, n in ((many, plan.slots), (few, plan.slots - 1)):

        @pl.when(cond)
        def _():
            wait_for(wo.at[0, :, pl.ds(0, n * nd)], o_recv)

    sp_o.start(lambda to: wo.at[d])
    for s in range(r):
        wait_for(wd.at[d, s], d_recv.at[s])
    sp_d.start(lambda to: wd.at[d])
    for s in range(2, plan.nc):
        ag_x.step(s)
    for s in range(1, plan.nc):
        ag_c.step(s)

    ag_x.finish()
    ag_c.finish()
    for sp in (sp_v, sp_s, sp_q, sp_o, sp_d, sp_u):
        sp.wait()
        sp.wait_sent()
    wait_for(vec_own, loc.at[0])
    wait_for(seg_own, loc.at[1])
    wait_for(wu_own, loc.at[2])

    def sent_q(j, carry):
        g = q * per_dev + j
        third = g // per_third
        head = (g - third * per_third) // nq

        @pl.when(plan.owner(head) != q)
        def _():
            wait_for(wq_own.at[0], q_send.at[j])

        return carry

    lax.fori_loop(0, per_dev, sent_q, 0)

    def sent_o(j, carry):
        to = plan.owner((d * HEADS + j) // nd)

        @pl.when(jnp.logical_not((q // r == d) & (to == q)))
        def _():
            wait_for(wo_own.at[0], o_send.at[j])

        return carry

    lax.fori_loop(0, HEADS, sent_o, 0)
    for s in range(r):

        @pl.when(jnp.logical_not((q // r == d) & (d * r + s == q)))
        def _():
            wait_for(wd_own.at[s], d_send.at[s])


def start_call(plan, x, c, vec, seg, wq, wo, wu, wd):
    nd, nq, r = plan.nd, plan.nq, plan.ratio
    shape = jax.ShapeDtypeStruct
    outs = (
        shape((nq, *x.shape), x.dtype),
        shape((nq, *c.shape), c.dtype),
        shape((nq, *vec.shape), vec.dtype),
        shape((nq, *seg.shape), seg.dtype),
        shape((nd, plan.groups_q, plan.gq, plan.kd), BF16),
        shape((nd, r, plan.groups_o, plan.go, plan.cq), BF16),
        shape((nd, *wu.shape), BF16),
        shape((nd, *wd.shape), BF16),
    )
    return pl.pallas_call(
        functools.partial(start_kernel, plan),
        out_shape=outs,
        in_specs=[VMEM] * 8,
        out_specs=[ANY] * 8,
        scratch_shapes=[
            pltpu.VMEM((nq, plan.gq, plan.kd), BF16),
            pltpu.VMEM((nd, plan.go, plan.cq), BF16),
            *Gather.sems(plan),
            *Gather.sems(plan),
            dma(3 + r),
            dma(nq),
            dma(nq),
            dma(nq),
            dma(nq),
            dma(3 * HEADS),
            pltpu.SemaphoreType.DMA,
            dma(nd),
            dma(nd),
            dma(HEADS),
            pltpu.SemaphoreType.DMA,
            dma(nd),
            dma(nd),
            dma(r),
            dma(r),
            dma(nd),
            dma(nd),
            dma(nd),
            dma(nd),
        ],
        compiler_params=pltpu.CompilerParams(
            collective_id=0, has_side_effects=True, vmem_limit_bytes=VMEM_LIMIT
        ),
        name="start",
    )(x, c, vec, seg, wq, wo, wu, wd)


def gather_kernel(plan, own, buf, *sem):
    greet_chain(plan)
    ag = Gather(plan, own, buf, *sem)
    ag.start()
    for s in range(1, plan.nc):
        ag.step(s)
    ag.finish()


def gather_call(plan, own, ident):
    return pl.pallas_call(
        functools.partial(gather_kernel, plan),
        out_shape=jax.ShapeDtypeStruct((plan.nq, *own.shape), own.dtype),
        in_specs=[VMEM],
        out_specs=ANY,
        scratch_shapes=Gather.sems(plan),
        compiler_params=pltpu.CompilerParams(
            collective_id=ident, has_side_effects=True, vmem_limit_bytes=VMEM_LIMIT
        ),
        name="gather",
    )(own)


def scatter_kernel(plan, n, *refs):
    parts, outs, scratch = refs[:n], refs[n : 2 * n], refs[2 * n :]
    greet_chain(plan)
    each = len(scratch) // n
    rs = [
        Scatter(plan, parts[i], *scratch[i * each : i * each + 3], scratch[i * each + 3 : (i + 1) * each])
        for i in range(n)
    ]
    for one in rs:
        one.start()
    for one in rs:
        one.flows()
    for one, out in zip(rs, outs):
        one.finish(out)


def scatter_call(plan, parts, ident):
    n = len(parts)
    return pl.pallas_call(
        functools.partial(scatter_kernel, plan, n),
        out_shape=[jax.ShapeDtypeStruct((plan.tl, plan.width), F32)] * n,
        in_specs=[VMEM] * n,
        out_specs=[VMEM] * n,
        scratch_shapes=Scatter.scratch(plan) * n,
        compiler_params=pltpu.CompilerParams(
            collective_id=ident, has_side_effects=True, vmem_limit_bytes=VMEM_LIMIT
        ),
        name="scatter",
    )(*parts)


def end_kernel(plan, *refs):
    (p_n1, g_u, g_d, g_q, g_o) = refs[:5]
    (out_n1, r_u, o_d, o_q, o_o) = refs[5:10]
    (r_d, r_q, r_o, s_d, s_q, s_o) = refs[10:16]
    swap, flow, run, *rest = refs[16:]
    rs_sems, sem = rest[:4], rest[4:]
    d, q = here()
    nd, nq, r = plan.nd, plan.nq, plan.ratio
    it = iter(sem)
    sp = [Spread(plan, "dp", buf, next(it), next(it)) for buf in (r_u, r_d, r_q, r_o)]
    loc = next(it)
    d_send, d_recv, q_send, q_recv, o_send, o_recv = (next(it) for _ in range(6))
    rs = Scatter(plan, p_n1, swap, flow, run, rs_sems)

    greet_all(plan)
    rs.start()
    parts = (g_u, g_d, g_q, g_o)
    for i in (1, 2, 3, 0):
        sp[i].start(lambda to, i=i: parts[i].at[to])
        local(parts[i].at[d], sp[i].buf.at[d], loc.at[i]).start()
    rs.flows()

    sp[1].wait()
    wait_for(r_d.at[d], loc.at[1])
    for s in range(r):
        total = r_d[0, s].astype(F32)
        for i in range(1, nd):
            total += r_d[i, s].astype(F32)
        s_d[s] = total.astype(BF16)
        to_d, to_q = q // r, d * r + s
        mine = (to_d == d) & (to_q == q)
        move(
            s_d.at[s], o_d.at[lax.rem(q, r)], d_send.at[s], d_recv.at[lax.rem(q, r)], to_d, to_q, mine
        )

    per_third = HEADS * nq
    per_dev = 3 * HEADS
    sp[2].wait()
    wait_for(r_q.at[d], loc.at[2])
    first, count = plan.first(q), plan.count(q)

    def qkv_group(k, carry):
        total = r_q[0, k].astype(F32)
        for i in range(1, nd):
            total += r_q[i, k].astype(F32)
        s_q[k] = total.astype(BF16)
        return carry

    lax.fori_loop(0, plan.groups_q, qkv_group, 0)

    def qkv_place(k):
        third = k // (plan.slots * nq)
        rest = k - third * (plan.slots * nq)
        slot = rest // nq
        g = third * per_third + first * nq + rest
        to = g // per_dev
        return slot, to, g - to * per_dev

    def qkv_send(k, carry):
        slot, to, j = qkv_place(k)

        @pl.when(slot < count)
        def _():
            move(s_q.at[k], o_q.at[j], q_send.at[k], q_recv, d, to, to == q)

        return carry

    lax.fori_loop(0, plan.groups_q, qkv_send, 0)

    sp[3].wait()
    wait_for(r_o.at[d], loc.at[3])

    def out_place(k):
        slot = k // nd
        g = first * nd + k
        to_d = g // HEADS
        return slot, to_d, g - to_d * HEADS

    for s in range(r):

        def out_group(k, carry):
            total = r_o[0, s, k].astype(F32)
            for i in range(1, nd):
                total += r_o[i, s, k].astype(F32)
            s_o[s, k] = total.astype(BF16)
            return carry

        lax.fori_loop(0, plan.groups_o, out_group, 0)

    for s in range(r):

        def out_send(k, carry):
            slot, to_d, j = out_place(k)
            to_q = d * r + s
            mine = (to_d == d) & (to_q == q)

            @pl.when(slot < count)
            def _():
                move(s_o.at[s, k], o_o.at[j], o_send.at[s, k], o_recv, to_d, to_q, mine)

            return carry

        lax.fori_loop(0, plan.groups_o, out_send, 0)

    sp[0].wait()
    wait_for(r_u.at[d], loc.at[0])
    rs.finish(out_n1)
    for s in range(r):
        wait_for(o_d.at[s], d_recv.at[s])
    wait_for(o_q, q_recv)
    wait_for(o_o, o_recv)
    for one in sp:
        one.wait_sent()

    for s in range(r):

        @pl.when(jnp.logical_not((q // r == d) & (d * r + s == q)))
        def _():
            wait_for(s_d.at[s], d_send.at[s])

    def sent_q(k, carry):
        slot, to, j = qkv_place(k)

        @pl.when((slot < count) & (to != q))
        def _():
            wait_for(s_q.at[0], q_send.at[k])

        return carry

    lax.fori_loop(0, plan.groups_q, sent_q, 0)
    for s in range(r):

        def sent_o(k, carry):
            slot, to_d, j = out_place(k)
            mine = (to_d == d) & (d * r + s == q)

            @pl.when((slot < count) & jnp.logical_not(mine))
            def _():
                wait_for(s_o.at[0, 0], o_send.at[s, k])

            return carry

        lax.fori_loop(0, plan.groups_o, sent_o, 0)


def end_call(plan, p_n1, g_u, g_d, g_q, g_o, ident):
    nd, nq, r = plan.nd, plan.nq, plan.ratio
    shape = jax.ShapeDtypeStruct
    return pl.pallas_call(
        functools.partial(end_kernel, plan),
        out_shape=(
            shape((plan.tl, plan.width), F32),
            shape(g_u.shape, BF16),
            shape(g_d.shape[1:], BF16),
            shape((3 * HEADS, plan.gq, plan.kd), BF16),
            shape((HEADS, plan.go, plan.cq), BF16),
        ),
        in_specs=[VMEM, ANY, ANY, ANY, ANY],
        out_specs=[VMEM, ANY, ANY, ANY, ANY],
        scratch_shapes=[
            pltpu.VMEM(g_d.shape, BF16),
            pltpu.VMEM(g_q.shape, BF16),
            pltpu.VMEM(g_o.shape, BF16),
            pltpu.VMEM(g_d.shape[1:], BF16),
            pltpu.VMEM(g_q.shape[1:], BF16),
            pltpu.VMEM(g_o.shape[1:], BF16),
            *Scatter.scratch(plan),
            *[dma(nd)] * 8,
            dma(4),
            dma(r),
            dma(r),
            dma(plan.groups_q),
            pltpu.SemaphoreType.DMA,
            dma(r, plan.groups_o),
            pltpu.SemaphoreType.DMA,
        ],
        compiler_params=pltpu.CompilerParams(
            collective_id=ident, has_side_effects=True, vmem_limit_bytes=VMEM_LIMIT
        ),
        name="end",
    )(p_n1, g_u, g_d, g_q, g_o)


def vector_kernel(plan, v_own, u_own, v_out, u_out, r_seq, r_dp, r_u, mid, *sem):
    d, q = here()
    greet_all(plan)
    it = iter(sem)
    sp_s = Spread(plan, "seq", r_seq, next(it), next(it))
    sp_d = Spread(plan, "dp", r_dp, next(it), next(it))
    sp_u = Spread(plan, "dp", r_u, next(it), next(it))
    sp_u.start(lambda to: u_own)
    sp_s.start(lambda to: v_own.at[to])
    sp_s.wait()
    total = v_own[q]
    for k in range(1, plan.nq):
        total += r_seq[sp_s.other(k)]
    mid[...] = total
    sp_d.start(lambda to: mid)
    sp_u.wait()
    sum_u = u_own[...]
    for k in range(1, plan.nd):
        sum_u += r_u[sp_u.other(k)]
    u_out[...] = sum_u
    sp_d.wait()
    for k in range(1, plan.nd):
        total += r_dp[sp_d.other(k)]
    v_out[...] = total
    for one in (sp_s, sp_d, sp_u):
        one.wait_sent()


def vector_call(plan, v, u, ident):
    nd, nq = plan.nd, plan.nq
    shape = jax.ShapeDtypeStruct
    return pl.pallas_call(
        functools.partial(vector_kernel, plan),
        out_shape=(shape(v.shape[1:], F32), shape(u.shape, F32)),
        in_specs=[VMEM] * 2,
        out_specs=[VMEM] * 2,
        scratch_shapes=[
            pltpu.VMEM(v.shape, F32),
            pltpu.VMEM((nd, *v.shape[1:]), F32),
            pltpu.VMEM((nd, *u.shape), F32),
            pltpu.VMEM(v.shape[1:], F32),
            dma(nq),
            dma(nq),
            dma(nd),
            dma(nd),
            dma(nd),
            dma(nd),
        ],
        compiler_params=pltpu.CompilerParams(
            collective_id=ident, has_side_effects=True, vmem_limit_bytes=VMEM_LIMIT
        ),
        name="vectors",
    )(v, u)


ROWS = 256


def visible(segc, segr, at, start, rows, keys):
    seen = segc[at : at + rows] == segr[:, start : start + keys]
    qpos = at + lax.broadcasted_iota(jnp.int32, (rows, keys), 0)
    kpos = start + lax.broadcasted_iota(jnp.int32, (rows, keys), 1)
    return seen & (kpos <= qpos)


def only(half, values):
    lane = lax.broadcasted_iota(jnp.int32, values.shape, 1)
    keep = (lane < HEAD_DIM) if half == 0 else (lane >= HEAD_DIM)
    return jnp.where(keep, values, jnp.zeros_like(values))


def either(first, second):
    lane = lax.broadcasted_iota(jnp.int32, first.shape, 1)
    return jnp.where(lane < HEAD_DIM, first, second)


def attend_kernel(plan, q_ref, k_ref, v_ref, segc, segr, o_ref, lse_ref):
    length, most = plan.length, plan.length // 2
    for at in range(0, length, ROWS):
        start = max(0, at - most)
        keys = at + ROWS - start
        mask = visible(segc, segr, at, start, ROWS, keys)
        query = q_ref[at : at + ROWS]
        key, value = k_ref[start : start + keys], v_ref[start : start + keys]
        outs, logs = [], []
        for half in range(2):
            scores = dot(only(half, query), key, NT) * (HEAD_DIM**-0.5)
            scores = jnp.where(mask, scores, -1e30)
            top = jnp.max(scores, axis=-1, keepdims=True)
            weights = jnp.exp(scores - top)
            total = jnp.sum(weights, axis=-1, keepdims=True)
            probs = (weights * (1.0 / total)).astype(BF16)
            outs.append(dot(probs, value, NN))
            logs.append(jnp.broadcast_to(top + jnp.log(total), (ROWS, 2 * HEAD_DIM)))
        o_ref[at : at + ROWS] = either(*outs).astype(BF16)
        lse_ref[at : at + ROWS] = either(*logs)


def attend_call(plan, mixed, segc, segr):
    pairs = plan.slots // 2
    block = lambda third: pl.BlockSpec((plan.length, 128), lambda i: (0, third * pairs + i))
    whole = lambda a: pl.BlockSpec(a.shape, lambda i: (0, 0))
    return pl.pallas_call(
        functools.partial(attend_kernel, plan),
        grid=(pairs,),
        out_shape=(
            jax.ShapeDtypeStruct((plan.length, plan.hw), BF16),
            jax.ShapeDtypeStruct((plan.length, plan.hw), F32),
        ),
        in_specs=[block(0), block(1), block(2), whole(segc), whole(segr)],
        out_specs=[block(0), block(0)],
        compiler_params=pltpu.CompilerParams(vmem_limit_bytes=VMEM_LIMIT),
        name="attend",
    )(mixed, mixed, mixed, segc, segr)


def attend_back_kernel(plan, q_ref, k_ref, v_ref, g_ref, lse_ref, segc, segr, dq, dk, dv, ak, av):
    length, most = plan.length, plan.length // 2
    scaling = HEAD_DIM**-0.5
    ak[...] = jnp.zeros_like(ak)
    av[...] = jnp.zeros_like(av)
    for at in range(0, length, ROWS):
        start = max(0, at - most)
        keys = at + ROWS - start
        mask = visible(segc, segr, at, start, ROWS, keys)
        query, grad = q_ref[at : at + ROWS], g_ref[at : at + ROWS]
        key, value = k_ref[start : start + keys], v_ref[start : start + keys]
        outs = []
        for half in range(2):
            query_h, grad_h = only(half, query), only(half, grad)
            scores = dot(query_h, key, NT) * scaling
            scores = jnp.where(mask, scores, -1e30)
            log = lse_ref[at : at + ROWS, half * HEAD_DIM : half * HEAD_DIM + 1]
            probs = jnp.exp(scores - log)
            grad_probs = dot(grad_h, value, NT)
            delta = jnp.sum(probs * grad_probs, axis=-1, keepdims=True)
            grad_scores = (probs * (grad_probs - delta)).astype(BF16)
            outs.append(dot(grad_scores, key, NN))
            ak[start : start + keys] += dot(grad_scores, query_h, TN)
            av[start : start + keys] += dot(probs.astype(BF16), grad_h, TN)
        dq[at : at + ROWS] = (either(*outs) * scaling).astype(BF16)
    dk[...] = (ak[...] * scaling).astype(BF16)
    dv[...] = av[...].astype(BF16)


def attend_back_call(plan, mixed, grad, lse, segc, segr):
    pairs = plan.slots // 2
    block = lambda third: pl.BlockSpec((plan.length, 128), lambda i: (0, third * pairs + i))
    whole = lambda a: pl.BlockSpec(a.shape, lambda i: (0, 0))
    return pl.pallas_call(
        functools.partial(attend_back_kernel, plan),
        grid=(pairs,),
        out_shape=[jax.ShapeDtypeStruct((plan.length, plan.hw), BF16)] * 3,
        in_specs=[block(0), block(1), block(2), block(0), block(0), whole(segc), whole(segr)],
        out_specs=[block(0)] * 3,
        scratch_shapes=[pltpu.VMEM((plan.length, 128), F32)] * 2,
        compiler_params=pltpu.CompilerParams(vmem_limit_bytes=VMEM_LIMIT),
        name="attend_back",
    )(mixed, mixed, mixed, grad, lse, segc, segr)


def shards(
    nd,
    nq,
    inputs,
    segment_ids,
    cotangent,
    attn_gain,
    attn_shift,
    qkv_weight,
    query_bias,
    value_bias,
    out_weight,
    out_bias,
    mlp_gain,
    mlp_shift,
    up_weight,
    up_bias,
    down_weight,
    down_bias,
):
    width = inputs.shape[2]
    plan = Plan(nd, nq, inputs.shape[1], width, up_weight.shape[1] * nq)
    r, slots, length = plan.ratio, plan.slots, plan.length
    q = lax.axis_index("seq")
    first, count = plan.first(q), plan.count(q)

    vec = jnp.stack(
        [attn_gain, attn_shift, query_bias, value_bias, out_bias, mlp_gain, mlp_shift, down_bias]
    )
    got = start_call(
        plan,
        inputs[0],
        cotangent[0],
        vec,
        segment_ids,
        qkv_weight.T.reshape(3 * HEADS, plan.gq, plan.kd),
        out_weight.reshape(HEADS, plan.go, plan.cq),
        up_weight,
        down_weight.T.reshape(plan.cq, r, plan.fq).transpose(1, 0, 2),
    )
    gx, gc, gv, gs, wq, wo, wu, wd = got
    xs = gx.reshape(length, width).astype(F32)
    cot = gc.reshape(length, width)
    v = gv.transpose(1, 0, 2).reshape(8, width).astype(F32)
    gain_one, shift_one, bias_query, bias_value, bias_out, gain_two, shift_two, bias_down = v
    segr = gs.reshape(1, length)
    segc = gs.reshape(length, 1)
    wq = wq.reshape(nd, 3 * plan.hw, plan.kd).transpose(1, 0, 2).reshape(3 * plan.hw, width)
    wo = wo.reshape(nd, r, plan.hw, plan.cq).transpose(2, 0, 1, 3).reshape(plan.hw, width)
    wu = wu.reshape(width, plan.fq)
    wd = wd.reshape(width, plan.fq)

    normed = layer_norm(xs, gain_one, shift_one).astype(BF16)
    mine = lambda b: lax.dynamic_slice(jnp.pad(b, (0, plan.hw)), (first * HEAD_DIM,), (plan.hw,))
    biases = jnp.concatenate([mine(bias_query), jnp.zeros((plan.hw,), F32), mine(bias_value)])
    mixed = (dot(normed, wq, NT) + biases).astype(BF16)
    attended, lse = attend_call(plan, mixed, segc, segr)
    part = dot(attended, wo, NN).astype(BF16).reshape(nq, plan.tl, width)
    (branch,) = scatter_call(plan, [part], 1)
    stream = inputs[0].astype(F32)
    residual = stream + branch + bias_out
    second = layer_norm(residual, gain_two, shift_two).astype(BF16)
    second_all = gather_call(plan, second, 2).reshape(length, width)
    hidden = dot(second_all, wu, NN) + up_bias.astype(F32)
    activated = gelu_tanh(hidden).astype(BF16)
    part_out = dot(activated, wd, NT).astype(BF16).reshape(nq, plan.tl, width)
    grad_act = dot(cot, wd, NN)
    grad_hidden = jax.vjp(gelu_tanh, hidden)[1](grad_act)[0].astype(BF16)
    part_second = dot(grad_hidden, wu, NT).astype(BF16).reshape(nq, plan.tl, width)
    down_sum, grad_second = scatter_call(plan, [part_out, part_second], 3)
    output = residual + down_sum + bias_down

    grad_resid, grad_gain_two, grad_shift_two = jax.vjp(layer_norm, residual, gain_two, shift_two)[
        1
    ](grad_second)
    top = cotangent[0].astype(F32)
    grad_resid = grad_resid + top
    grad_branch = grad_resid.astype(BF16)
    branch_all = gather_call(plan, grad_branch, 4).reshape(length, width)
    grad_attended = dot(branch_all, wo, NT).astype(BF16)
    dq, dk, dv = attend_back_call(plan, mixed, grad_attended, lse, segc, segr)
    grad_mixed = jnp.concatenate([dq, dk, dv], axis=1)
    part_one = dot(grad_mixed, wq, NN).astype(BF16).reshape(nq, plan.tl, width)

    g_u = dot(second_all, grad_hidden, TN).astype(BF16).reshape(nd, plan.kd, plan.fq)
    g_d = dot(cot, activated, TN).astype(BF16).reshape(nd, r, plan.cq, plan.fq)
    g_q = dot(grad_mixed, normed, TN).astype(BF16).reshape(3 * plan.hw, nd, plan.kd)
    g_q = g_q.transpose(1, 0, 2).reshape(nd, plan.groups_q, plan.gq, plan.kd)
    g_o = dot(attended, branch_all, TN).astype(BF16).reshape(plan.hw, nd, r, plan.cq)
    g_o = g_o.transpose(1, 2, 0, 3).reshape(nd, r, plan.groups_o, plan.go, plan.cq)
    grad_normed, r_u, o_d, o_q, o_o = end_call(plan, part_one, g_u, g_d, g_q, g_o, 5)
    grad_stream, grad_gain_one, grad_shift_one = jax.vjp(layer_norm, stream, gain_one, shift_one)[
        1
    ](grad_normed)
    grad_input = grad_stream + grad_resid

    def spread_heads(grad):
        sums = jnp.sum(grad.astype(F32), axis=0)
        sums = jnp.where(jnp.arange(plan.hw) < count * HEAD_DIM, sums, 0.0)
        full = jnp.zeros((width + plan.hw,), F32)
        return lax.dynamic_update_slice(full, sums, (first * HEAD_DIM,))[:width]

    vectors = jnp.stack(
        [
            grad_gain_one,
            grad_shift_one,
            spread_heads(dq),
            spread_heads(dv),
            jnp.sum(grad_branch.astype(F32), axis=0),
            grad_gain_two,
            grad_shift_two,
            jnp.sum(top, axis=0),
        ]
    )
    vectors = vectors.reshape(8, nq, plan.cq).transpose(1, 0, 2)
    up_sum = jnp.sum(grad_hidden.astype(F32), axis=0)[None]
    vectors, up_sum = vector_call(plan, vectors, up_sum, 6)
    grad_up = jnp.sum(r_u.astype(F32), axis=0)
    grad_down = o_d.astype(F32).transpose(0, 2, 1).reshape(r * plan.fq, plan.cq)
    grad_qkv = o_q.astype(F32).reshape(3 * HEADS * plan.gq, plan.kd).T
    grad_out = o_o.astype(F32).reshape(plan.kd, plan.cq)
    return (
        output.astype(BF16)[None],
        grad_input[None],
        vectors[0],
        vectors[1],
        grad_qkv,
        vectors[2],
        vectors[3],
        grad_out,
        vectors[4],
        vectors[5],
        vectors[6],
        grad_up,
        up_sum[0],
        grad_down,
        vectors[7],
    )


def solution(mesh):
    tokens, vector, matrix = P("dp", "seq", None), P("seq"), P("dp", "seq")
    return jax.shard_map(
        functools.partial(shards, mesh.shape["dp"], mesh.shape["seq"]),
        mesh=mesh,
        in_specs=(
            tokens,
            matrix,
            tokens,
            vector,
            vector,
            matrix,
            vector,
            vector,
            matrix,
            vector,
            vector,
            vector,
            matrix,
            vector,
            matrix,
            vector,
        ),
        out_specs=(
            tokens,
            tokens,
            vector,
            vector,
            matrix,
            vector,
            vector,
            matrix,
            vector,
            vector,
            vector,
            matrix,
            vector,
            matrix,
            vector,
        ),
        check_vma=False,
    )
```

time: 2920 us -> 726 us (0.25)
  waiting for transfers between devices: 2230 us -> 0 us
  Pallas kernels: 0 us -> 555 us
  local copies, waits for them, and re-layouts: 337 us -> 69.8 us
  matrix products: 211 us -> 58.7 us
  blocking collectives: 73.5 us -> 0 us
    unnamed x26 -> x0, waiting for transfers between devices: 1060 us -> none
    all_gather x9 -> x0, waiting for transfers between devices: 622 us -> none  [the longest x1 184 us: shards(): lax.all_gather(rows[2], 'seq', axis=1, tiled=True)]
    pallas_call x0 -> x9, Pallas kernels: none -> 555 us  [the longest x1 159 us: end_call(): pl.pallas_call(functools.partial(end_kernel, plan), out_shape=(shape((pla...]
    reduce_scatter x3 -> x0, waiting for transfers between devices: 545 us -> none  [the longest x1 412 us: shards(): lax.psum_scatter(local_mats[2], 'seq', scatter_dimension=1, tiled=True)]
    dynamic_update_slice x8 -> x0, local copies, waits for them, and re-layouts: 248 us -> none  [shards(): lax.scan(grad_step, jnp.zeros((tok_count, HEADS, HEAD_DIM), jnp.float32),...]
    dot_general x30 -> x12, matrix products: 211 us -> 58.7 us  [dot(): lax.dot_general(left, right, (dims, ((), ())), preferred_element_type=F32)]
    unnamed x149 -> x48, local copies, waits for them, and re-layouts: 59.4 us -> 6.45 us
    unnamed x1 -> x0, blocking collectives: 31.6 us -> none
  transfers between devices with their start and end apart: 19 -> 0, of which waited for: 19 -> 0; matrix products, arithmetic and copies ran while one was open for 7% -> 0% of each run, Pallas kernels for 0% -> 0%
where the time goes in v1:
time: 726 us; the launch traced here: 713 us
  Pallas kernels  555 us (76%)
  local copies, waits for them, and re-layouts  69.8 us (10%)
  matrix products  58.7 us (8%)
  other arithmetic  27.2 us (4%)
    pallas_call x1, Pallas kernels, end_call(): pl.pallas_call(functools.partial(end_kernel, plan), out_shape=(shape((pla...  159 us
    pallas_call x1, Pallas kernels, start_call(): pl.pallas_call(functools.partial(start_kernel, plan), out_shape=outs, in_...  150 us
    pallas_call x2, Pallas kernels, scatter_call(): pl.pallas_call(functools.partial(scatter_kernel, plan, n), out_shape=[jax...  140 us
    pallas_call x2, Pallas kernels, gather_call(): pl.pallas_call(functools.partial(gather_kernel, plan), out_shape=jax.Shap...  70.3 us
    dot_general x12, matrix products, dot(): lax.dot_general(left, right, (dims, ((), ())), preferred_element_type=F32)  58.7 us

profile of v1, /device:TPU:2, one launch (start us, length us, event | category | flops | bytes accessed | tf_op | source)
XLA Modules:
  0.0 712.8 jit_solution(16036151301920789232)
XLA Ops:
  7.3 2.0 copy.45
  9.3 2.0 copy.46
  11.2 2.1 copy.47
  15.0 150.1 %start.1 = (bf16[8,128,1600]{2,1,0:T(8,128)(2,1)}, bf16[8,128,1600]{2,1,0:T(8,128)(2,1)}, bf16[8,8,200]{2,1,0:T(8,128)(2,1)}, s32[8,1,128]{2,1,0:T(1,128)}, bf16...) custom-call(bf16[128,1600]{1,0:T(8,128)(2,1)} %bitcast.118, ...), custom_call_target="tpu_custom_call" | custom-call | tf_op jit(solution)/shard_map/start/pallas_call | solution.py:508
  165.1 4.6 copy.49
  173.4 2.2 copy.51
  175.6 2.8 fusion.3
  178.3 1.5 add_convert_fusion
  180.0 4.1 add_convert_fusion.1.q_ref.k_ref.v_ref
  184.1 10.1 %attend.1 = (bf16[1024,256]{1,0:T(8,128)(2,1)}, f32[1024,256]{1,0:T(8,128)}) custom-call(bf16[1024,768]{1,0:T(8,128)(2,1)} %add_convert_fusion.1.q_ref.k_ref.v_ref, bf16[1024,768]{1,0:T(8,128)(2,1)} %add_convert_fusion.1.q_ref.k_ref.v_ref, bf16[1024,768]{1,0:T(8,128)(2,1)} %add_convert_fusion.1.q_ref.k_ref.v_ref, s32[1024,1]{1,0:T(8,128)} %copy.50.segc, ...), custom_call_target="tpu_custom_call" | custom-call | tf_op jit(solution)/shard_map/attend/pallas_call | solution.py:884
  194.2 2.4 convolution_convert_fusion.3
  196.6 3.7 copy.52
  200.2 62.1 %scatter.2 = f32[128,1600]{1,0:T(8,128)} custom-call(bf16[8,128,1600]{2,1,0:T(8,128)(2,1)} %bitcast.119), custom_call_target="tpu_custom_call" | custom-call | tf_op jit(solution)/shard_map/scatter/pallas_call | solution.py:586
  262.4 1.4 fusion.31
  265.0 35.2 %gather.2 = bf16[8,128,1600]{2,1,0:T(8,128)(2,1)} custom-call(bf16[128,1600]{1,0:T(8,128)(2,1)} %add_convert_fusion.3.own), custom_call_target="tpu_custom_call" | custom-call | tf_op jit(solution)/shard_map/gather/pallas_call | solution.py:555
  300.3 6.2 fusion.34
  306.6 6.0 convert_reduce_fusion.2
  312.6 5.4 convolution_convert_fusion.4
  318.0 5.6 convolution_convert_fusion.1
  323.6 4.5 convolution_convert_fusion.5
  328.7 5.4 copy.53
  334.1 5.2 copy.57
  339.4 5.2 copy.58
  344.6 7.6 %convolution_convert_fusion = bf16[1024,1600]{0,1:T(8,128)(2,1)} fusion(bf16[1600,800]{1,0:T(8,128)(2,1)} %bitcast.164, bf16[1024,800]{0,1:T(8,128)(2,1)} %copy-done.20), kind=kOutput, calls=%fused_computation.11 | convolution fusion | flops 2623078400 | bytes 7475200 | tf_op jit(solution)/shard_map/dot_general | solution.py:32
  352.2 5.4 copy.54
  357.6 77.6 %scatter.3 = (f32[128,1600]{1,0:T(8,128)}, f32[128,1600]{1,0:T(8,128)}) custom-call(bf16[8,128,1600]{2,1,0:T(8,128)(2,1)} %bitcast.120, bf16[8,128,1600]{2,1,0:T(8,128)(2,1)} %bitcast.122), custom_call_target="tpu_custom_call" | custom-call | tf_op jit(solution)/shard_map/scatter/pallas_call | solution.py:586
  435.3 1.6 multiply_reduce_fusion.1
  437.0 1.8 fusion.30
  441.0 35.0 %gather.3 = bf16[8,128,1600]{2,1,0:T(8,128)(2,1)} custom-call(bf16[128,1600]{1,0:T(8,128)(2,1)} %get-tuple-element.108.own), custom_call_target="tpu_custom_call" | custom-call | tf_op jit(solution)/shard_map/gather/pallas_call | solution.py:555
  476.1 4.0 convolution_convert_fusion.8.g_ref
  480.1 2.4 convolution_convert_fusion.7
  482.5 13.4 %attend_back.1 = (bf16[1024,256]{1,0:T(8,128)(2,1)}, bf16[1024,256]{1,0:T(8,128)(2,1)}, bf16[1024,256]{1,0:T(8,128)(2,1)}) custom-call(bf16[1024,768]{1,0:T(8,128)(2,1)} %add_convert_fusion.1.q_ref.k_ref.v_ref, bf16[1024,768]{1,0:T(8,128)(2,1)} %add_convert_fusion.1.q_ref.k_ref.v_ref, bf16[1024,768]{1,0:T(8,128)(2,1)} %add_convert_fusion.1.q_ref.k_ref.v_ref, ...), custom_call_target="tpu_custom_call" | custom-call | tf_op jit(solution)/shard_map/attend_back/pallas_call | solution.py:931
  495.9 1.3 convert_reduce_fusion.6
  499.1 2.2 copy.60
  501.5 6.4 convolution_convert_fusion.6
  507.9 4.1 convolution_convert_fusion.2
  512.0 5.4 copy.56
  517.4 4.5 copy.59
  522.0 159.1 %end.1 = (f32[128,1600]{1,0:T(8,128)}, bf16[4,400,800]{2,1,0:T(8,128)(2,1)}, bf16[2,200,800]{2,1,0:T(8,128)(2,1)}, bf16[75,8,400]{2,1,0:T(8,128)(2,1)}, bf16[25,16,200]{2,1,0:T(8,128)(2,1)}) custom-call(bf16[8,128,1600]{2,1,0:T(8,128)(2,1)} %bitcast.121, bf16[4,400,800]{2,1,0:T(8,128)(2,1)} %bitcast.124, bf16[4,2,200,800]{3,2,1,0:T(8,128)(2,1)} %bitcast.125, ...), custom_call_target="tpu_custom_call" | custom-call | tf_op jit(solution)/shard_map/end/pallas_call | solution.py:747
  681.1 1.6 fusion.27
  682.8 1.6 fusion.18
  685.2 12.6 %vectors.1 = (f32[8,200]{1,0:T(8,128)}, f32[1,800]{1,0:T(1,128)}) custom-call(f32[8,8,200]{2,1,0:T(8,128)} %bitcast.146, f32[1,800]{1,0:T(1,128)} %broadcast_in_dim.44.u_own), custom_call_target="tpu_custom_call" | custom-call | tf_op jit(solution)/shard_map/vectors/pallas_call | solution.py:813
  697.9 1.6 fusion.33
  701.7 1.7 bitcast_convert_fusion.1
  703.4 1.2 bitcast_convert_fusion
  704.6 1.3 copy.61
  706.0 3.5 convert_reduce_fusion.1
  710.3 2.0 reshape.304
  (106 shorter events, 22.2 us)
Async XLA Ops:
  0.6 12.7 %copy-start.13 = (bf16[1600,200]{0,1:T(8,128)(2,1)S(1)}, bf16[1600,200]{0,1:T(8,128)(2,1)}, u32[]{:S(2)}) copy-start(bf16[1600,200]{0,1:T(8,128)(2,1)} %param.30) | copy-start | bytes 1920004
  165.1 4.6 copy-start
  169.7 1.6 copy-start.16
  169.7 2.6 copy-start.15
  178.3 1.7 copy-start.7
  200.2 62.1 %copy-start.1 = (bf16[1,128,1600]{2,1,0:T(8,128)(2,1)S(1)}, bf16[1,128,1600]{2,1,0:T(8,128)(2,1)}, u32[]{:S(2)}) copy-start(bf16[1,128,1600]{2,1,0:T(8,128)(2,1)} %copy.45) | copy-start | bytes 1228804
  300.3 6.3 copy-start.18
  300.3 6.3 copy-start.19
  312.6 11.0 %copy-start.20 = (bf16[1024,800]{0,1:T(8,128)(2,1)}, bf16[1024,800]{0,1:T(8,128)(2,1)S(1)}, u32[]{:S(2)}) copy-start(bf16[1024,800]{0,1:T(8,128)(2,1)S(1)} %get-tuple-element.106) | copy-start | bytes 4915204
  318.0 5.6 copy-start.4
  435.3 4.6 copy-start.3
  438.8 37.3 %copy-start.6 = (bf16[4,2,256,200]{2,3,1,0:T(8,128)(2,1)S(1)}, bf16[4,2,256,200]{2,3,1,0:T(8,128)(2,1)}, u32[]{:S(2)}) copy-start(bf16[4,2,256,200]{2,3,1,0:T(8,128)(2,1)} %copy.51) | copy-start | bytes 2457604
  476.1 4.0 copy-start.5
  476.1 4.0 copy-start.11
  495.9 5.4 copy-start.10
  495.9 5.5 copy-start.14
  495.9 5.5 copy-start.9
  501.5 6.4 copy-start.8
  681.1 18.4 %copy-start.2 = (f32[128,1600]{1,0:T(8,128)S(1)}, f32[128,1600]{1,0:T(8,128)}, u32[]{:S(2)}) copy-start(f32[128,1600]{1,0:T(8,128)} %get-tuple-element.52) | copy-start | bytes 2457604
  697.9 3.2 copy-start.17
  704.6 4.8 copy-start.12

commit v2 on v1

--- a/solution.py
+++ b/solution.py
@@ -116,6 +116,30 @@
     pl.semaphore_wait(barrier, 1 + jnp.minimum(chip, 1) + jnp.minimum(plan.nc - 1 - chip, 1))
 
 
+def greet_near(plan):
+    d, q = here()
+    chip, core = q // CORES, lax.rem(q, CORES)
+    barrier = pltpu.get_barrier_semaphore()
+    signal(barrier, d, q + 1 - 2 * core)
+
+    @pl.when(chip < plan.nc - 1)
+    def _():
+        signal(barrier, d, q + CORES)
+
+    @pl.when(chip > 0)
+    def _():
+        signal(barrier, d, q - CORES)
+
+    for k in range(1, plan.nd):
+        signal(barrier, lax.rem(d + k, plan.nd), q)
+    near = jnp.minimum(chip, 1) + jnp.minimum(plan.nc - 1 - chip, 1)
+    pl.semaphore_wait(barrier, near + plan.nd)
+
+
+def dma(*shape):
+    return pltpu.SemaphoreType.DMA(shape)
+
+
 class Gather:
     def __init__(self, plan, own, buf, send, recv, loc):
         self.plan, self.own, self.buf, self.send, self.recv, self.loc = plan, own, buf, send, recv, loc
@@ -149,33 +173,44 @@
         self.push(self.own, self.chip, 2).start()
         local(self.own, self.buf.at[self.q], self.loc).start()
 
+    def arrive(self, origin):
+        slot = origin * CORES + self.core
+        wait_for(self.buf.at[slot], self.recv.at[slot])
+
+        @pl.when((origin < self.chip) & (self.chip < self.plan.nc - 1))
+        def _():
+            self.push(self.buf.at[slot], origin, 0).start()
+
+        @pl.when((origin > self.chip) & (self.chip > 0))
+        def _():
+            self.push(self.buf.at[slot], origin, 1).start()
+
+        self.push(self.buf.at[slot], origin, 2).start()
+
     def step(self, s):
+        @pl.when(self.chip >= s)
+        def _():
+            self.arrive(self.chip - s)
+
+        @pl.when(self.chip + s < self.plan.nc)
+        def _():
+            self.arrive(self.chip + s)
+
+    def wait_own(self):
+        wait_for(self.own, self.loc)
+
+    def wait_partner(self, origin):
+        slot = origin * CORES + 1 - self.core
+        wait_for(self.buf.at[slot], self.recv.at[slot])
+
+    def finish(self):
+        self.wait_own()
+        for o in range(self.plan.nc):
+            self.wait_partner(o)
+        self.sent()
+
+    def sent(self):
         nc = self.plan.nc
-
-        def arrive(origin, way):
-            slot = origin * CORES + self.core
-            wait_for(self.buf.at[slot], self.recv.at[slot])
-
-            @pl.when((self.chip < nc - 1) if way == 0 else (self.chip > 0))
-            def _():
-                self.push(self.buf.at[slot], origin, way).start()
-
-            self.push(self.buf.at[slot], origin, 2).start()
-
-        @pl.when(self.chip >= s)
-        def _():
-            arrive(self.chip - s, 0)
-
-        @pl.when(self.chip + s < nc)
-        def _():
-            arrive(self.chip + s, 1)
-
-    def finish(self):
-        nc = self.plan.nc
-        wait_for(self.own, self.loc)
-        for o in range(nc):
-            slot = o * CORES + 1 - self.core
-            wait_for(self.buf.at[slot], self.recv.at[slot])
         for o in range(nc):
             wait_for(self.own, self.send.at[2, o])
 
@@ -327,10 +362,6 @@
             wait_for(self.buf.at[self.me], self.send.at[k])
 
 
-def dma(*shape):
-    return pltpu.SemaphoreType.DMA(shape)
-
-
 def move(src, dst, send, recv, d, q, mine):
     @pl.when(jnp.logical_not(mine))
     def _():
@@ -339,6 +370,299 @@
     @pl.when(mine)
     def _():
         local(src, dst, recv).start()
+
+
+class Flow:
+    def __init__(self, plan, part, run, swap, flow, s_swap, r_swap, s_flow, r_flow):
+        self.plan, self.part, self.run, self.swap, self.flow = plan, part, run, swap, flow
+        self.s_swap, self.r_swap, self.s_flow, self.r_flow = s_swap, r_swap, s_flow, r_flow
+        self.d, self.q = here()
+        self.chip, self.core = self.q // CORES, lax.rem(self.q, CORES)
+
+    @staticmethod
+    def scratch(plan):
+        block, nc = (plan.tl, plan.width), plan.nc
+        return [
+            pltpu.VMEM((nc, *block), BF16),
+            pltpu.VMEM((nc, *block), BF16),
+            pltpu.VMEM((nc, *block), BF16),
+            pltpu.VMEM((nc + 1, *block), BF16),
+            dma(nc),
+            dma(nc),
+            dma(nc),
+            dma(nc + 1),
+        ]
+
+    def put(self, o, values):
+        low, high = values[: self.plan.tl], values[self.plan.tl :]
+        mine = self.core == 0
+        self.run[o] = jnp.where(mine, low, high).astype(BF16)
+        self.part[o] = jnp.where(mine, high, low).astype(BF16)
+        remote(
+            self.part.at[o],
+            self.swap.at[o],
+            self.s_swap.at[o],
+            self.r_swap.at[o],
+            self.d,
+            self.q + 1 - 2 * self.core,
+        ).start()
+
+    def forward(self, o):
+        plan, chip = self.plan, self.chip
+        up = o > chip
+        inner = jnp.where(up, chip > 0, chip < plan.nc - 1)
+        to_chip = jnp.where(up, chip + 1, chip - 1)
+        slot = jnp.where(jnp.logical_not(up) & (o == to_chip), plan.nc, o)
+        wait_for(self.swap.at[o], self.r_swap.at[o])
+
+        @pl.when(inner)
+        def _():
+            wait_for(self.flow.at[o], self.r_flow.at[o])
+            total = self.run[o].astype(F32) + self.swap[o].astype(F32) + self.flow[o].astype(F32)
+            self.run[o] = total.astype(BF16)
+
+        @pl.when(jnp.logical_not(inner))
+        def _():
+            self.run[o] = (self.run[o].astype(F32) + self.swap[o].astype(F32)).astype(BF16)
+
+        remote(
+            self.run.at[o],
+            self.flow.at[slot],
+            self.s_flow.at[o],
+            self.r_flow.at[slot],
+            self.d,
+            to_chip * CORES + self.core,
+        ).start()
+
+    def passes(self, which, near_first, skip=None):
+        plan, chip = self.plan, self.chip
+        up = (chip * 2 < plan.nc) if which == 0 else (chip * 2 >= plan.nc)
+
+        def one(i, carry):
+            k = i if near_first else plan.nc - 1 - i
+            o = jnp.where(up, k, plan.nc - 1 - k)
+            go = jnp.where(up, o > chip, o < chip)
+            if skip is not None:
+                go = go & jnp.logical_not(skip(o))
+
+            @pl.when(go)
+            def _():
+                self.forward(o)
+
+            return carry
+
+        lax.fori_loop(0, plan.nc, one, 0)
+
+    def finish(self, out):
+        plan, nc, chip = self.plan, self.plan.nc, self.chip
+        wait_for(self.swap.at[chip], self.r_swap.at[chip])
+        out[...] = self.run[chip].astype(F32) + self.swap[chip].astype(F32)
+
+        @pl.when(chip > 0)
+        def _():
+            wait_for(self.flow.at[chip], self.r_flow.at[chip])
+            out[...] += self.flow[chip].astype(F32)
+
+        @pl.when(chip < nc - 1)
+        def _():
+            wait_for(self.flow.at[nc], self.r_flow.at[nc])
+            out[...] += self.flow[nc].astype(F32)
+
+    def sent(self):
+        for o in range(self.plan.nc):
+            wait_for(self.swap.at[o], self.s_swap.at[o])
+
+            @pl.when(self.chip != o)
+            def _():
+                wait_for(self.run.at[o], self.s_flow.at[o])
+
+
+def nearest(plan, t):
+    chip = lax.axis_index("seq") // CORES
+    below, above = chip, plan.nc - 1 - chip
+    both = jnp.minimum(below, above)
+    s = jnp.where(t <= 2 * both, (t + 1) // 2, t - both)
+    down = jnp.where(t <= 2 * both, lax.rem(t, 2) == 1, below > above)
+    return jnp.where(down, chip - s, chip + s)
+
+
+def norm_back(values, gain, grad):
+    center = values - jnp.mean(values, axis=-1, keepdims=True)
+    spread = jnp.mean(center * center, axis=-1, keepdims=True)
+    inverse = lax.rsqrt(spread + 1e-05)
+    hat = center * inverse
+    scaled = grad * gain
+    inner = jnp.mean(scaled, axis=-1, keepdims=True)
+    outer = jnp.mean(scaled * hat, axis=-1, keepdims=True)
+    back = (scaled - inner - hat * outer) * inverse
+    return back, jnp.sum(grad * hat, axis=0, keepdims=True), jnp.sum(grad, axis=0, keepdims=True)
+
+
+ROOT = 0.7978845608028654
+CUBE = 0.044715
+
+
+def gelu_both(h):
+    t = jnp.tanh(ROOT * (h + CUBE * (h * h * h)))
+    half = 0.5 * (1.0 + t)
+    slope = half + 0.5 * h * (1.0 - t * t) * (ROOT * (1.0 + 3.0 * CUBE * (h * h)))
+    return h * half, slope
+
+
+LANES = 512
+
+
+def mlp_kernel(plan, *refs):
+    (n_own, resid, c_own, cot, wu, wd, rows, ub) = refs[:8]
+    (out, gres, branch, r_u, r_d, vec, up_sum) = refs[8:15]
+    (n2, act, gh, gu, gd, br, tmp) = refs[15:22]
+    rest = list(refs[22:])
+    d, q = here()
+    nc, nd, tl, kd = plan.nc, plan.nd, plan.tl, plan.kd
+    chip = q // CORES
+    take = lambda n: [rest.pop(0) for _ in range(n)]
+    ag = Gather(plan, n_own, n2, *take(3))
+    ag_b = Gather(plan, br, branch, *take(3))
+    rs = Flow(plan, *take(8))
+    rs_o = Flow(plan, *take(8))
+    sp_u = Spread(plan, "dp", r_u, *take(2))
+    sp_d = Spread(plan, "dp", r_d, *take(2))
+    (loc,) = take(1)
+    greet_near(plan)
+    ag.start()
+    up_sum[...] = jnp.zeros_like(up_sum)
+    end_chip = (chip == 0) | (chip == nc - 1)
+
+    def process(o):
+        both = pl.ds(o * CORES, CORES)
+        x = n2[both].reshape(CORES * tl, plan.width)
+        h = dot(x, wu[...], NN) + ub[...]
+        value, slope = gelu_both(h)
+        value = value.astype(BF16)
+        c = cot[both].reshape(CORES * tl, plan.width)
+        g = (dot(c, wd[...], NN) * slope).astype(BF16)
+        act[both] = value.reshape(CORES, tl, plan.fq)
+        gh[both] = g.reshape(CORES, tl, plan.fq)
+        up_sum[...] += jnp.sum(g.astype(F32), axis=0, keepdims=True)
+        rs.put(o, dot(g, wu[...], NT))
+
+    def step(t, carry):
+        o = nearest(plan, t)
+
+        @pl.when(t > 0)
+        def _():
+            ag.arrive(o)
+
+        @pl.when(t == 0)
+        def _():
+            ag.wait_own()
+
+        ag.wait_partner(o)
+        process(o)
+
+        @pl.when(end_chip & (t >= 2))
+        def _():
+            rs.forward(nearest(plan, t - 1))
+
+        return carry
+
+    lax.fori_loop(0, nc, step, 0)
+    last = nearest(plan, nc - 1)
+
+    @pl.when(end_chip)
+    def _():
+        rs.forward(last)
+
+    def weight_grad(left, right, buf, sp, sem):
+        for at in range(0, plan.width, LANES):
+            n = min(LANES, plan.width - at)
+            a = left[:, :, at : at + n].reshape(plan.length, n)
+            b = right[...].reshape(plan.length, plan.fq)
+            buf[at : at + n] = dot(a, b, TN).astype(BF16)
+        rows_of = lambda i: buf.at[pl.ds(pl.multiple_of(i * kd, 8), kd)]
+        sp.start(rows_of)
+        local(rows_of(d), sp.buf.at[d], sem).start()
+
+    weight_grad(n2, gh, gu, sp_u, loc.at[0])
+    done = lambda o: end_chip
+    rs.passes(0, True, done)
+    weight_grad(cot, act, gd, sp_d, loc.at[1])
+    rs.passes(1, True, done)
+    rs.finish(tmp)
+
+    back, g_gain, g_shift = norm_back(resid[...], rows[0:1], tmp[...])
+    total = back + c_own[...].astype(F32)
+    gres[...] = total
+    low = total.astype(BF16)
+    br[...] = low
+    ag_b.start()
+    vec[0:1] = g_gain
+    vec[1:2] = g_shift
+    vec[2:3] = jnp.sum(low.astype(F32), axis=0, keepdims=True)
+
+    def down(t, carry):
+        o = nearest(plan, nc - 1 - t)
+        a = act[pl.ds(o * CORES, CORES)].reshape(CORES * tl, plan.fq)
+        rs_o.put(o, dot(a, wd[...], NT))
+        return carry
+
+    lax.fori_loop(0, nc, down, 0)
+    ag_b.step(1)
+    rs_o.passes(0, False)
+    for s in range(2, nc):
+        ag_b.step(s)
+    rs_o.passes(1, False)
+    rs_o.finish(tmp)
+    out[...] = (resid[...] + tmp[...] + rows[1:2]).astype(BF16)
+    ag_b.finish()
+    ag.sent()
+    rs.sent()
+    rs_o.sent()
+    for i, sp in enumerate((sp_u, sp_d)):
+        sp.wait()
+        sp.wait_sent()
+        wait_for(sp.buf.at[d], loc.at[i])
+
+
+def mlp_call(plan, n_own, resid, c_own, cot, wu, wd, rows, ub, ident):
+    shape = jax.ShapeDtypeStruct
+    nd, nq, tl, width, fq, kd = plan.nd, plan.nq, plan.tl, plan.width, plan.fq, plan.kd
+    return pl.pallas_call(
+        functools.partial(mlp_kernel, plan),
+        out_shape=(
+            shape((tl, width), BF16),
+            shape((tl, width), F32),
+            shape((nq, tl, width), BF16),
+            shape((nd, kd, fq), BF16),
+            shape((nd, kd, fq), BF16),
+            shape((3, width), F32),
+            shape((1, fq), F32),
+        ),
+        in_specs=[VMEM] * 8,
+        out_specs=[VMEM, VMEM, ANY, ANY, ANY, VMEM, VMEM],
+        scratch_shapes=[
+            pltpu.VMEM((nq, tl, width), BF16),
+            pltpu.VMEM((nq, tl, fq), BF16),
+            pltpu.VMEM((nq, tl, fq), BF16),
+            pltpu.VMEM((width, fq), BF16),
+            pltpu.VMEM((width, fq), BF16),
+            pltpu.VMEM((tl, width), BF16),
+            pltpu.VMEM((tl, width), F32),
+            *Gather.sems(plan),
+            *Gather.sems(plan),
+            *Flow.scratch(plan),
+            *Flow.scratch(plan),
+            dma(nd),
+            dma(nd),
+            dma(nd),
+            dma(nd),
+            dma(2),
+        ],
+        compiler_params=pltpu.CompilerParams(
+            collective_id=ident, has_side_effects=True, vmem_limit_bytes=VMEM_LIMIT
+        ),
+        name="mlp",
+    )(n_own, resid, c_own, cot, wu, wd, rows, ub)
 
 
 def start_kernel(plan, *refs):
@@ -597,44 +921,37 @@
 
 
 def end_kernel(plan, *refs):
-    (p_n1, g_u, g_d, g_q, g_o) = refs[:5]
-    (out_n1, r_u, o_d, o_q, o_o) = refs[5:10]
-    (r_d, r_q, r_o, s_d, s_q, s_o) = refs[10:16]
-    swap, flow, run, *rest = refs[16:]
+    (p_n1, s_d, g_q, g_o) = refs[:4]
+    (out_n1, o_d, o_q, o_o) = refs[4:8]
+    (r_q, r_o, s_q, s_o) = refs[8:12]
+    swap, flow, run, *rest = refs[12:]
     rs_sems, sem = rest[:4], rest[4:]
     d, q = here()
     nd, nq, r = plan.nd, plan.nq, plan.ratio
     it = iter(sem)
-    sp = [Spread(plan, "dp", buf, next(it), next(it)) for buf in (r_u, r_d, r_q, r_o)]
+    sp = [Spread(plan, "dp", buf, next(it), next(it)) for buf in (r_q, r_o)]
     loc = next(it)
     d_send, d_recv, q_send, q_recv, o_send, o_recv = (next(it) for _ in range(6))
     rs = Scatter(plan, p_n1, swap, flow, run, rs_sems)
 
     greet_all(plan)
     rs.start()
-    parts = (g_u, g_d, g_q, g_o)
-    for i in (1, 2, 3, 0):
+    parts = (g_q, g_o)
+    for i in (0, 1):
         sp[i].start(lambda to, i=i: parts[i].at[to])
         local(parts[i].at[d], sp[i].buf.at[d], loc.at[i]).start()
-    rs.flows()
-
-    sp[1].wait()
-    wait_for(r_d.at[d], loc.at[1])
     for s in range(r):
-        total = r_d[0, s].astype(F32)
-        for i in range(1, nd):
-            total += r_d[i, s].astype(F32)
-        s_d[s] = total.astype(BF16)
         to_d, to_q = q // r, d * r + s
         mine = (to_d == d) & (to_q == q)
         move(
             s_d.at[s], o_d.at[lax.rem(q, r)], d_send.at[s], d_recv.at[lax.rem(q, r)], to_d, to_q, mine
         )
 
+    rs.flows()
     per_third = HEADS * nq
     per_dev = 3 * HEADS
-    sp[2].wait()
-    wait_for(r_q.at[d], loc.at[2])
+    sp[0].wait()
+    wait_for(r_q.at[d], loc.at[0])
     first, count = plan.first(q), plan.count(q)
 
     def qkv_group(k, carry):
@@ -665,8 +982,8 @@
 
     lax.fori_loop(0, plan.groups_q, qkv_send, 0)
 
-    sp[3].wait()
-    wait_for(r_o.at[d], loc.at[3])
+    sp[1].wait()
+    wait_for(r_o.at[d], loc.at[1])
 
     def out_place(k):
         slot = k // nd
@@ -700,8 +1017,6 @@
 
         lax.fori_loop(0, plan.groups_o, out_send, 0)
 
-    sp[0].wait()
-    wait_for(r_u.at[d], loc.at[0])
     rs.finish(out_n1)
     for s in range(r):
         wait_for(o_d.at[s], d_recv.at[s])
@@ -741,30 +1056,27 @@
         lax.fori_loop(0, plan.groups_o, sent_o, 0)
 
 
-def end_call(plan, p_n1, g_u, g_d, g_q, g_o, ident):
+def end_call(plan, p_n1, g_d, g_q, g_o, ident):
     nd, nq, r = plan.nd, plan.nq, plan.ratio
     shape = jax.ShapeDtypeStruct
     return pl.pallas_call(
         functools.partial(end_kernel, plan),
         out_shape=(
             shape((plan.tl, plan.width), F32),
-            shape(g_u.shape, BF16),
-            shape(g_d.shape[1:], BF16),
+            shape(g_d.shape, BF16),
             shape((3 * HEADS, plan.gq, plan.kd), BF16),
             shape((HEADS, plan.go, plan.cq), BF16),
         ),
-        in_specs=[VMEM, ANY, ANY, ANY, ANY],
-        out_specs=[VMEM, ANY, ANY, ANY, ANY],
+        in_specs=[VMEM, ANY, ANY, ANY],
+        out_specs=[VMEM, ANY, ANY, ANY],
         scratch_shapes=[
-            pltpu.VMEM(g_d.shape, BF16),
             pltpu.VMEM(g_q.shape, BF16),
             pltpu.VMEM(g_o.shape, BF16),
-            pltpu.VMEM(g_d.shape[1:], BF16),
             pltpu.VMEM(g_q.shape[1:], BF16),
             pltpu.VMEM(g_o.shape[1:], BF16),
             *Scatter.scratch(plan),
-            *[dma(nd)] * 8,
-            dma(4),
+            *[dma(nd)] * 4,
+            dma(2),
             dma(r),
             dma(r),
             dma(plan.groups_q),
@@ -776,7 +1088,7 @@
             collective_id=ident, has_side_effects=True, vmem_limit_bytes=VMEM_LIMIT
         ),
         name="end",
-    )(p_n1, g_u, g_d, g_q, g_o)
+    )(p_n1, g_d, g_q, g_o)
 
 
 def vector_kernel(plan, v_own, u_own, v_out, u_out, r_seq, r_dp, r_u, mid, *sem):
@@ -1002,35 +1314,23 @@
     stream = inputs[0].astype(F32)
     residual = stream + branch + bias_out
     second = layer_norm(residual, gain_two, shift_two).astype(BF16)
-    second_all = gather_call(plan, second, 2).reshape(length, width)
-    hidden = dot(second_all, wu, NN) + up_bias.astype(F32)
-    activated = gelu_tanh(hidden).astype(BF16)
-    part_out = dot(activated, wd, NT).astype(BF16).reshape(nq, plan.tl, width)
-    grad_act = dot(cot, wd, NN)
-    grad_hidden = jax.vjp(gelu_tanh, hidden)[1](grad_act)[0].astype(BF16)
-    part_second = dot(grad_hidden, wu, NT).astype(BF16).reshape(nq, plan.tl, width)
-    down_sum, grad_second = scatter_call(plan, [part_out, part_second], 3)
-    output = residual + down_sum + bias_down
-
-    grad_resid, grad_gain_two, grad_shift_two = jax.vjp(layer_norm, residual, gain_two, shift_two)[
-        1
-    ](grad_second)
+    rows = jnp.stack([gain_two, bias_down])
+    output, grad_resid, branch_all, r_u, r_d, sums, up_sum = mlp_call(
+        plan, second, residual, cotangent[0], gc, wu, wd, rows, up_bias.astype(F32)[None], 2
+    )
     top = cotangent[0].astype(F32)
-    grad_resid = grad_resid + top
-    grad_branch = grad_resid.astype(BF16)
-    branch_all = gather_call(plan, grad_branch, 4).reshape(length, width)
+    branch_all = branch_all.reshape(length, width)
     grad_attended = dot(branch_all, wo, NT).astype(BF16)
     dq, dk, dv = attend_back_call(plan, mixed, grad_attended, lse, segc, segr)
     grad_mixed = jnp.concatenate([dq, dk, dv], axis=1)
     part_one = dot(grad_mixed, wq, NN).astype(BF16).reshape(nq, plan.tl, width)
 
-    g_u = dot(second_all, grad_hidden, TN).astype(BF16).reshape(nd, plan.kd, plan.fq)
-    g_d = dot(cot, activated, TN).astype(BF16).reshape(nd, r, plan.cq, plan.fq)
     g_q = dot(grad_mixed, normed, TN).astype(BF16).reshape(3 * plan.hw, nd, plan.kd)
     g_q = g_q.transpose(1, 0, 2).reshape(nd, plan.groups_q, plan.gq, plan.kd)
     g_o = dot(attended, branch_all, TN).astype(BF16).reshape(plan.hw, nd, r, plan.cq)
     g_o = g_o.transpose(1, 2, 0, 3).reshape(nd, r, plan.groups_o, plan.go, plan.cq)
-    grad_normed, r_u, o_d, o_q, o_o = end_call(plan, part_one, g_u, g_d, g_q, g_o, 5)
+    g_d = jnp.sum(r_d.astype(F32), axis=0).astype(BF16).reshape(r, plan.cq, plan.fq)
+    grad_normed, o_d, o_q, o_o = end_call(plan, part_one, g_d, g_q, g_o, 5)
     grad_stream, grad_gain_one, grad_shift_one = jax.vjp(layer_norm, stream, gain_one, shift_one)[
         1
     ](grad_normed)
@@ -1048,21 +1348,20 @@
             grad_shift_one,
             spread_heads(dq),
             spread_heads(dv),
-            jnp.sum(grad_branch.astype(F32), axis=0),
-            grad_gain_two,
-            grad_shift_two,
+            sums[2],
+            sums[0],
+            sums[1],
             jnp.sum(top, axis=0),
         ]
     )
     vectors = vectors.reshape(8, nq, plan.cq).transpose(1, 0, 2)
-    up_sum = jnp.sum(grad_hidden.astype(F32), axis=0)[None]
     vectors, up_sum = vector_call(plan, vectors, up_sum, 6)
     grad_up = jnp.sum(r_u.astype(F32), axis=0)
     grad_down = o_d.astype(F32).transpose(0, 2, 1).reshape(r * plan.fq, plan.cq)
     grad_qkv = o_q.astype(F32).reshape(3 * HEADS * plan.gq, plan.kd).T
     grad_out = o_o.astype(F32).reshape(plan.kd, plan.cq)
     return (
-        output.astype(BF16)[None],
+        output[None],
         grad_input[None],
         vectors[0],
         vectors[1],

time: 726 us -> 600 us (0.83)
  Pallas kernels: 555 us -> 485 us
  matrix products: 58.7 us -> 27.1 us
  local copies, waits for them, and re-layouts: 69.8 us -> 46.8 us
    pallas_call x2 -> x1, Pallas kernels: 140 us -> 62.1 us  [scatter_call(): pl.pallas_call(functools.partial(scatter_kernel, plan, n), out_shape=[jax...]
    pallas_call x2 -> x1, Pallas kernels: 70.3 us -> 133 us  [mlp_call(): pl.pallas_call(functools.partial(mlp_kernel, plan), out_shape=(shape((tl,...]
    pallas_call x1, Pallas kernels: 159 us -> 98.6 us  [end_call(): pl.pallas_call(functools.partial(end_kernel, plan), out_shape=(shape((pla...]
    dot_general x12 -> x6, matrix products: 58.7 us -> 27.1 us  [dot(): lax.dot_general(left, right, (dims, ((), ())), preferred_element_type=F32)]
    convert_element_type x4 -> x0, local copies, waits for them, and re-layouts: 21.3 us -> none  [the longest x1 5.44 us: shards(): part_out = dot(activated, wd, NT).astype(BF16).reshape(nq, plan.tl, width)]
where the time goes in v2:
time: 600 us; the launch traced here: 589 us
  Pallas kernels  485 us (81%)
  local copies, waits for them, and re-layouts  46.8 us (8%)
  other arithmetic  28.6 us (5%)
  matrix products  27.1 us (5%)
    pallas_call x1, Pallas kernels, start_call(): pl.pallas_call(functools.partial(start_kernel, plan), out_shape=outs, in_...  150 us
    pallas_call x1, Pallas kernels, mlp_call(): pl.pallas_call(functools.partial(mlp_kernel, plan), out_shape=(shape((tl,...  133 us
    pallas_call x1, Pallas kernels, end_call(): pl.pallas_call(functools.partial(end_kernel, plan), out_shape=(shape((pla...  98.6 us
    pallas_call x1, Pallas kernels, scatter_call(): pl.pallas_call(functools.partial(scatter_kernel, plan, n), out_shape=[jax...  62.1 us
    dot_general x6, matrix products, dot(): lax.dot_general(left, right, (dims, ((), ())), preferred_element_type=F32)  27.1 us
    pallas_call x1, Pallas kernels, vector_call(): pl.pallas_call(functools.partial(vector_kernel, plan), out_shape=(shape(v...  17.4 us
    pallas_call x1, Pallas kernels, attend_back_call(): pl.pallas_call(functools.partial(attend_back_kernel, plan), grid=(pairs,)...  13.4 us

profile of v2, /device:TPU:2, one launch (start us, length us, event | category | flops | bytes accessed | tf_op | source)
XLA Modules:
  0.0 589.4 jit_solution(3323842826595816051)
XLA Ops:
  0.8 2.1 copy.41
  2.9 2.0 copy.42
  4.8 2.3 reshape.234
  7.2 0.9 copy.59
  8.1 1.1 copy.43
  9.9 150.1 %start.1 = (bf16[8,128,1600]{2,1,0:T(8,128)(2,1)}, bf16[8,128,1600]{2,1,0:T(8,128)(2,1)}, bf16[8,8,200]{2,1,0:T(8,128)(2,1)}, s32[8,1,128]{2,1,0:T(1,128)}, bf16...) custom-call(bf16[128,1600]{1,0:T(8,128)(2,1)} %bitcast.99, ...), custom_call_target="tpu_custom_call" | custom-call | tf_op jit(solution)/shard_map/start/pallas_call | solution.py:832
  160.0 0.9 convert_bitcast_fusion.1
  161.4 2.5 convert_reduce_fusion
  163.9 1.0 multiply_reduce_fusion
  165.2 2.7 add_convert_fusion
  167.8 4.5 copy.45
  172.3 6.9 %add_convert_fusion.1.q_ref.k_ref.v_ref = bf16[1024,768]{1,0:T(8,128)(2,1)} fusion(bf16[1024,1600]{1,0:T(8,128)(2,1)} %bitcast.106, bf16[768,1600]{0,1:T(8,128)(2,1)} %bitcast.115, f32[768]{0:T(1024)S(1)} %pad_maximum_fusion.1), kind=kOutput, calls=%fused_computation.12 | convolution fusion | flops 2518155264 | bytes 7310336 | tf_op jit(solution)/shard_map/dot_general | solution.py:32
  179.2 1.0 copy.46.segc
  180.2 10.1 %attend.1 = (bf16[1024,256]{1,0:T(8,128)(2,1)}, f32[1024,256]{1,0:T(8,128)}) custom-call(bf16[1024,768]{1,0:T(8,128)(2,1)} %add_convert_fusion.1.q_ref.k_ref.v_ref, bf16[1024,768]{1,0:T(8,128)(2,1)} %add_convert_fusion.1.q_ref.k_ref.v_ref, bf16[1024,768]{1,0:T(8,128)(2,1)} %add_convert_fusion.1.q_ref.k_ref.v_ref, s32[1024,1]{1,0:T(8,128)} %copy.46.segc, ...), custom_call_target="tpu_custom_call" | custom-call | tf_op jit(solution)/shard_map/attend/pallas_call | solution.py:1196
  190.4 2.7 copy.47
  193.1 4.1 convolution_convert_fusion.1
  197.1 5.4 copy.48
  202.6 62.1 %scatter.1 = f32[128,1600]{1,0:T(8,128)} custom-call(bf16[8,128,1600]{2,1,0:T(8,128)(2,1)} %bitcast.101), custom_call_target="tpu_custom_call" | custom-call | tf_op jit(solution)/shard_map/scatter/pallas_call | solution.py:910
  264.8 1.5 fusion.18
  266.3 0.9 copy-done.2
  267.6 2.2 add_convert_fusion.2.refs_0_
  271.2 133.4 %mlp.1 = (bf16[128,1600]{1,0:T(8,128)(2,1)}, f32[128,1600]{1,0:T(8,128)}, bf16[8,128,1600]{2,1,0:T(8,128)(2,1)}, bf16[4,400,800]{2,1,0:T(8,128)(2,1)}, bf16[4,40...) custom-call(bf16[128,1600]{1,0:T(8,128)(2,1)} %add_convert_fusion.2.refs_0_, f32[128,1600]{1,0:T(8,128)} %copy-done.2, ...), custom_call_target="tpu_custom_call" | custom-call | tf_op jit(solution)/shard_map/mlp/pallas_call | solution.py:630
  404.7 4.3 convolution_convert_fusion.3
  409.0 2.4 copy.52
  411.4 4.1 convolution_convert_fusion.4.g_ref
  415.5 13.4 %attend_back.1 = (bf16[1024,256]{1,0:T(8,128)(2,1)}, bf16[1024,256]{1,0:T(8,128)(2,1)}, bf16[1024,256]{1,0:T(8,128)(2,1)}) custom-call(bf16[1024,768]{1,0:T(8,128)(2,1)} %add_convert_fusion.1.q_ref.k_ref.v_ref, bf16[1024,768]{1,0:T(8,128)(2,1)} %add_convert_fusion.1.q_ref.k_ref.v_ref, bf16[1024,768]{1,0:T(8,128)(2,1)} %add_convert_fusion.1.q_ref.k_ref.v_ref, ...), custom_call_target="tpu_custom_call" | custom-call | tf_op jit(solution)/shard_map/attend_back/pallas_call | solution.py:1243
  428.8 1.1 constant_dynamic-update-slice_fusion.2
  429.9 1.1 constant_dynamic-update-slice_fusion.1
  431.0 1.1 constant_dynamic-update-slice_fusion
  432.1 1.6 fusion.3
  433.7 2.9 convolution_convert_fusion.2
  436.6 3.0 copy.51
  439.6 4.9 convolution_convert_fusion
  444.5 3.6 copy.50
  448.2 3.3 reduce_sum.158
  451.5 98.6 %end.1 = (f32[128,1600]{1,0:T(8,128)}, bf16[2,200,800]{2,1,0:T(8,128)(2,1)}, bf16[75,8,400]{2,1,0:T(8,128)(2,1)}, bf16[25,16,200]{2,1,0:T(8,128)(2,1)}) custom-call(bf16[8,128,1600]{2,1,0:T(8,128)(2,1)} %bitcast.100, bf16[2,200,800]{2,1,0:T(8,128)(2,1)} %bitcast.110, bf16[4,96,8,400]{3,2,1,0:T(8,128)(2,1)} %bitcast.102, bf16[4,2,16,16,200]{4,3,2,1,0:T(8,128)(2,1)} %bitcast.105), custom_call_target="tpu_custom_call" | custom-call | tf_op jit(solution)/shard_map/end/pallas_call | solution.py:1062
  550.1 1.2 convert_bitcast_fusion
  552.1 2.0 reshape.261
  554.1 1.3 bitcast_convert_fusion
  555.4 1.3 copy.54
  557.8 1.2 convert_reduce_fusion.4
  560.8 17.4 %vectors.1 = (f32[8,200]{1,0:T(8,128)}, f32[1,800]{1,0:T(1,128)}) custom-call(f32[8,8,200]{2,1,0:T(8,128)} %bitcast.124, f32[1,800]{1,0:T(1,128)} %get-tuple-element.60.u_own), custom_call_target="tpu_custom_call" | custom-call | tf_op jit(solution)/shard_map/vectors/pallas_call | solution.py:1125
  578.2 1.6 fusion.20
  579.7 1.3 reduce.13
  581.0 1.5 add_bitcast_fusion
  582.5 1.2 copy.57
  584.5 3.5 convert_reduce_fusion.1
  588.0 0.9 copy.56
  (96 shorter events, 7.5 us)
Async XLA Ops:
  0.6 7.4 %copy-start.7 = (bf16[400,600]{1,0:T(8,128)(2,1)S(1)}, bf16[400,600]{1,0:T(8,128)(2,1)}, u32[]{:S(2)}) copy-start(bf16[400,600]{1,0:T(8,128)(2,1)} %param.21) | copy-start | bytes 1440004
  0.7 8.5 %copy-start.14 = (bf16[200]{0:T(256)(128)(2,1)S(1)}, bf16[200]{0:T(256)(128)(2,1)}, u32[]{:S(2)}) copy-start(bf16[200]{0:T(256)(128)(2,1)} %param.19) | copy-start | bytes 1204
  0.7 8.5 %copy-start.15 = (bf16[200]{0:T(256)(128)(2,1)S(1)}, bf16[200]{0:T(256)(128)(2,1)}, u32[]{:S(2)}) copy-start(bf16[200]{0:T(256)(128)(2,1)} %param.20) | copy-start | bytes 1204
  0.7 8.5 %copy-start.16 = (bf16[200]{0:T(256)(128)(2,1)S(1)}, bf16[200]{0:T(256)(128)(2,1)}, u32[]{:S(2)}) copy-start(bf16[200]{0:T(256)(128)(2,1)} %param.22) | copy-start | bytes 1204
  0.7 8.5 %copy-start.17 = (bf16[200]{0:T(256)(128)(2,1)S(1)}, bf16[200]{0:T(256)(128)(2,1)}, u32[]{:S(2)}) copy-start(bf16[200]{0:T(256)(128)(2,1)} %param.23) | copy-start | bytes 1204
  0.7 8.5 %copy-start.18 = (bf16[200]{0:T(256)(128)(2,1)S(1)}, bf16[200]{0:T(256)(128)(2,1)}, u32[]{:S(2)}) copy-start(bf16[200]{0:T(256)(128)(2,1)} %param.25) | copy-start | bytes 1204
  0.7 8.6 %copy-start.19 = (bf16[200]{0:T(256)(128)(2,1)S(1)}, bf16[200]{0:T(256)(128)(2,1)}, u32[]{:S(2)}) copy-start(bf16[200]{0:T(256)(128)(2,1)} %param.26) | copy-start | bytes 1204
  0.7 8.6 %copy-start.20 = (bf16[200]{0:T(256)(128)(2,1)S(1)}, bf16[200]{0:T(256)(128)(2,1)}, u32[]{:S(2)}) copy-start(bf16[200]{0:T(256)(128)(2,1)} %param.27) | copy-start | bytes 1204
  0.7 8.6 %copy-start.21 = (bf16[200]{0:T(256)(128)(2,1)S(1)}, bf16[200]{0:T(256)(128)(2,1)}, u32[]{:S(2)}) copy-start(bf16[200]{0:T(256)(128)(2,1)} %param.31) | copy-start | bytes 1204
  160.0 3.9 copy-start
  172.3 6.9 %copy-start.11 = (s32[8,1,128]{2,1,0:T(1,128)S(1)}, s32[8,1,128]{2,1,0:T(1,128)}, u32[]{:S(2)}) copy-start(s32[8,1,128]{2,1,0:T(1,128)} %get-tuple-element.44) | copy-start | bytes 12292
  202.6 68.0 %copy-start.13 = (bf16[800]{0:T(1024)(128)(2,1)S(1)}, bf16[800]{0:T(1024)(128)(2,1)}, u32[]{:S(2)}) copy-start(bf16[800]{0:T(1024)(128)(2,1)} %param.29) | copy-start | bytes 4804
  266.3 0.9 copy-start.2
  271.2 133.5 %copy-start.6 = (bf16[1024,256]{1,0:T(8,128)(2,1)S(1)}, bf16[1024,256]{1,0:T(8,128)(2,1)}, u32[]{:S(2)}) copy-start(bf16[1024,256]{1,0:T(8,128)(2,1)} %get-tuple-element.45) | copy-start | bytes 1572868
  432.1 1.6 copy-start.10
  552.1 4.7 copy-start.1
  552.1 4.7 copy-start.3
  554.1 5.1 copy-start.5
  555.4 4.2 copy-start.12
  555.4 4.5 copy-start.4
  557.6 26.1 %copy-start.9 = (bf16[25,16,200]{2,1,0:T(8,128)(2,1)S(1)}, bf16[25,16,200]{2,1,0:T(8,128)(2,1)}, u32[]{:S(2)}) copy-start(bf16[25,16,200]{2,1,0:T(8,128)(2,1)} %get-tuple-element.63) | copy-start | bytes 480004
  582.5 5.5 copy-start.8
